TPU v7x, 128 devices: a whole 4x4x4 slice. The times are simulated.
128 devices in a mesh: grp: 4 (over x), dev: 32 (over y, z, core).
Axes of the slice: x: 4, y: 4, z: 4, core: 2. Of those that a mesh axis runs over, the one named last changes fastest.
Arguments:
- basis: float32 [2048, 64, 1024], P(('grp', 'dev')), may hold values from -0.25 to 0.25
- leaf_transfer: float32 [2048, 4096], P(('grp', 'dev')), may hold values from -0.75 to 1.75
- upper_transfer: float32 [1024, 4096], P(('grp', 'dev')), may hold values from -0.75 to 1.75
- coupling: float32 [16384, 4096], P(('grp', 'dev')), may hold values from -6 to 6
- row_leaf: int32 [16384], P(('grp', 'dev')), may hold values from 0 to 15
- col_dev: int32 [16384, 1], P(('grp', 'dev')), may hold values from 0 to 127; in each aligned block of 128 rows (0 to 127, 128 to 255, ...) at most 2 rows name the same one
- col_leaf: int32 [16384], P(('grp', 'dev')), may hold values from 0 to 15
Outputs:
- ortho_basis: float32 [2048, 64, 1024], P(('grp', 'dev'))
- leaf_transfer_out: float32 [2048, 4096], P(('grp', 'dev'))
- upper_transfer_out: float32 [1024, 4096], P(('grp', 'dev'))
- coupling_out: float32 [16384, 4096], P(('grp', 'dev'))
Inputs may be any that keep to these rules, and one draw needn't show every extreme that they name: `col_dev`: among the 128 blocks of one device no device index appears more than 2 times, and some index appears exactly 2 times on some device.
All inputs are finite; a program needn't handle non-finite values.
Results may differ from a plain program's by a relative error of at most 0.0003.
Values sent between devices are 32-bit elements; how exact they have to be, the bound alone decides.
No kernel may reach another device: no remote copies, remote signals or barrier semaphores. Data moves between devices by JAX's collectives and lax.ppermute only.
A program may use at most 128 MiB of HBM per device.

v0:
```python
import math

import jax
import jax.numpy as jnp
from jax import lax
from jax.sharding import PartitionSpec as P

exact_mode = lax.Precision.HIGHEST


def from_partner(shard, axis, apart):
    return lax.ppermute(shard, axis, [(i, i ^ 1 << apart) for i in range(lax.axis_size(axis))])


def left_solve(lower, mats):
    return lax.linalg.triangular_solve(lower, mats, left_side=True, lower=True)


def right_solve(lower, mats):
    return lax.linalg.triangular_solve(lower, mats, left_side=False, lower=True, transpose_a=True)


def transpose_mul(first, second):
    return jnp.einsum("nji,njk->nik", first, second, precision=exact_mode)


def pick_rows(labels, table, leaves):
    chosen = (labels[..., None] == jnp.arange(leaves, dtype=labels.dtype)).astype(jnp.float32)
    return jnp.dot(chosen, table, precision=exact_mode)


def shards(basis, leaf_transfer, upper_transfer, coupling, row_leaf, col_dev, col_leaf):
    leaves, width, points = basis.shape
    gram = jnp.einsum("nkp,njp->nkj", basis, basis, precision=exact_mode)
    lower = jnp.linalg.cholesky(gram)
    ortho_basis = left_solve(lower, basis) * math.sqrt(points)
    lifted = transpose_mul(lower, leaf_transfer.reshape(leaves, width, width))
    inner = transpose_mul(lifted, lifted)
    lower_one = jnp.linalg.cholesky(inner.reshape(leaves // 2, 2, width, width).sum(axis=1))
    new_leaf = right_solve(jnp.repeat(lower_one, 2, axis=0), lifted)
    clusters = leaves // 2
    raised = transpose_mul(lower_one, upper_transfer.reshape(clusters, width, width))
    inner_up = transpose_mul(raised, raised)
    partner = from_partner(inner_up, "grp", 0)
    lower_two = jnp.linalg.cholesky(inner_up + partner)
    new_upper = right_solve(lower_two, raised)
    square = width * width
    upper_leaf = jnp.swapaxes(lower, 1, 2).reshape(leaves, square)
    blocks = coupling.shape[0]
    row_factor = pick_rows(row_leaf, upper_leaf, leaves).reshape(blocks, width, width)
    left = jnp.einsum(
        "bij,bjk->bik", row_factor, coupling.reshape(blocks, width, width), precision=exact_mode
    )
    owners = lax.axis_size(("grp", "dev"))
    slots = max(2, 2 * blocks // owners)
    dests = col_dev[:, 0]
    marks = (dests[:, None] == jnp.arange(owners, dtype=jnp.int32)[None, :]).astype(jnp.int32)
    places = jnp.sum(jnp.cumsum(marks, axis=0) * marks, axis=1) - 1
    outgoing = (
        jnp.zeros((owners, slots, square), jnp.float32)
        .at[dests, places]
        .set(left.reshape(blocks, square))
    )
    labels = (
        jnp.zeros((owners, slots), jnp.float32)
        .at[dests, places]
        .set(col_leaf.astype(jnp.float32) + 1.0)
    )
    arrived = lax.all_to_all(outgoing, ("grp", "dev"), split_axis=0, concat_axis=0, tiled=True)
    tags = lax.all_to_all(labels, ("grp", "dev"), split_axis=0, concat_axis=0, tiled=True)
    sources, count, _ = arrived.shape
    chosen = (tags[..., None] == jnp.arange(leaves, dtype=jnp.float32) + 1.0).astype(jnp.float32)
    factor = jnp.dot(chosen.reshape(-1, leaves), upper_leaf, precision=exact_mode)
    factor = factor.reshape(sources * count, width, width)
    finished = jnp.einsum(
        "bij,bkj->bik", arrived.reshape(sources * count, width, width), factor, precision=exact_mode
    )
    returned = lax.all_to_all(
        finished.reshape(sources, count, square),
        ("grp", "dev"),
        split_axis=0,
        concat_axis=0,
        tiled=True,
    )
    coupling_out = returned[dests, places]
    return (
        ortho_basis,
        new_leaf.reshape(leaves, square),
        new_upper.reshape(clusters, square),
        coupling_out,
    )


def solution(mesh):
    in_specs = (
        P(("grp", "dev"), None, None),
        P(("grp", "dev"), None),
        P(("grp", "dev"), None),
        P(("grp", "dev"), None),
        P(("grp", "dev")),
        P(("grp", "dev"), None),
        P(("grp", "dev")),
    )
    out_specs = (
        P(("grp", "dev"), None, None),
        P(("grp", "dev"), None),
        P(("grp", "dev"), None),
        P(("grp", "dev"), None),
    )
    return jax.shard_map(shards, mesh=mesh, in_specs=in_specs, out_specs=out_specs, check_vma=False)
```

profile of v0, /device:TPU:1, one launch (start us, length us, event | category | flops | bytes accessed | tf_op | source)
XLA Modules:
  0.0 602.5 jit_solution(9135050669245547209)
XLA Ops:
  3.7 6.4 %scatter_fusion.1 = f32[128,2]{0,1:T(2,128)S(1)} fusion(f32[128,2]{0,1:T(2,128)S(1)} %broadcast_in_dim.16, s32[128]{0:T(128)S(1)} %get-tuple-element.5, f32[128]{0:T(128)S(1)} %convert_add_fusion), kind=kCustom, calls=%fused_computation.2 | custom fusion | bytes 2560 | tf_op jit(solution)/shard_map/scatter | solution.py:67
  10.8 11.5 %all-to-all-start.1 = ((f32[128,1,2]{2,1,0:T(1,128)}), f32[128,1,2]{2,1,0:T(1,128)S(1)}, u32[]{:S(2)}, u32[]{:S(2)}) async-start(f32[128,1,2]{2,1,0:T(1,128)} %copy.103), calls=%async_computation.1 | async-start | bytes 131072 | tf_op jit(solution)/shard_map/all_to_all | solution.py:70
  22.3 7.4 %fusion.32 = f32[16,64,64]{2,1,0:T(8,128)S(1)} fusion(f32[16,64,1024]{2,1,0:T(8,128)} %param.8), kind=kOutput, calls=%fused_computation.61 | convolution fusion | flops 805306368 | bytes 4456448 | tf_op jit(solution)/shard_map/nkp,njp->nkj/dot_general | solution.py:34
  30.0 93.8 %custom-call.16 = f32[16,64,64]{2,1,0:T(8,128)S(1)} custom-call(f32[16,64,64]{2,1,0:T(8,128)S(1)} %fusion.3), custom_call_target="Cholesky" | custom-call | tf_op jit(solution)/shard_map/jit(cholesky)/cholesky | solution.py:35
  127.5 4.5 copy.99
  133.9 4.7 copy.100
  138.5 9.8 %fusion.35 = f32[128,64,64]{2,1,0:T(8,128)} fusion(f32[128,64,64]{2,1,0:T(8,128)} %copy.99, f32[128,64,64]{2,1,0:T(8,128)} %copy.100), kind=kOutput, calls=%fused_computation.64 | convolution fusion | flops 402653184 | bytes 6291456 | tf_op jit(solution)/shard_map/bij,bjk->bik/dot_general | solution.py:51
  148.4 4.8 copy.101
  155.1 4.1 broadcast_in_dim.15
  159.2 24.3 %scatter_fusion = f32[128,2,4096]{2,1,0:T(2,128)} fusion(f32[128,2,4096]{2,1,0:T(2,128)} %broadcast_in_dim.15, s32[128]{0:T(128)S(1)} %get-tuple-element.5, f32[128,4096]{1,0:T(8,128)S(1)} %copy.102), kind=kCustom, calls=%fused_computation.1 | custom fusion | bytes 6292480 | tf_op jit(solution)/shard_map/scatter | solution.py:62
  183.5 10.6 %all-to-all-start = ((f32[128,2,4096]{2,1,0:T(2,128)}), f32[128,2,4096]{2,1,0:T(2,128)}, u32[]{:S(2)}, u32[]{:S(2)}) async-start(f32[128,2,4096]{2,1,0:T(2,128)} %scatter_fusion), calls=%async_computation | async-start | bytes 8388608 | tf_op jit(solution)/shard_map/all_to_all | solution.py:69
  199.4 9.1 %copy.105 = f32[256,64,64]{2,1,0:T(8,128)} copy(f32[256,64,64]{0,2,1:T(8,128)} %fusion.4) | data formatting | bytes 8388608 | tf_op jit(solution)/shard_map/dot_general | solution.py:73
  208.6 38.0 %all-to-all-done = f32[128,2,4096]{2,1,0:T(2,128)} async-done(((f32[128,2,4096]{2,1,0:T(2,128)}), f32[128,2,4096]{2,1,0:T(2,128)}, u32[]{:S(2)}, u32[]{:S(2)}) %all-to-all-start) | async-done | bytes 4194336 | tf_op jit(solution)/shard_map/all_to_all | solution.py:69
  246.6 8.7 %reshape.120 = f32[256,64,64]{2,1,0:T(8,128)} reshape(f32[128,2,4096]{2,1,0:T(2,128)} %all-to-all-done) | data formatting | bytes 8388608 | tf_op jit(solution)/shard_map/reshape | solution.py:76
  255.3 19.2 %fusion.36 = f32[256,64,64]{2,1,0:T(8,128)} fusion(f32[256,64,64]{2,1,0:T(8,128)} %reshape.120, f32[256,64,64]{2,1,0:T(8,128)} %copy.105), kind=kOutput, calls=%fused_computation.65 | convolution fusion | flops 805306368 | bytes 12582912 | tf_op jit(solution)/shard_map/bij,bkj->bik/dot_general | solution.py:75
  274.5 8.8 %reshape.121 = f32[128,2,4096]{2,1,0:T(2,128)} reshape(f32[256,64,64]{2,1,0:T(8,128)} %fusion.36) | data formatting | bytes 8388608 | tf_op jit(solution)/shard_map/reshape | solution.py:79
  283.3 5.8 all-to-all-start.2
  291.7 46.9 %custom-call.27 = f32[8,64,64]{2,1,0:T(8,128)S(1)} custom-call(f32[8,64,64]{2,1,0:T(8,128)S(1)} %fusion.13), custom_call_target="Cholesky" | custom-call | tf_op jit(solution)/shard_map/jit(cholesky)/cholesky | solution.py:39
  341.8 78.8 %custom-call.18 = f32[16,1,64,64]{2,3,1,0:T(8,128)S(1)} custom-call(f32[16,1,64,64]{3,2,1,0:T(8,128)S(1)} %broadcast_select_fusion), custom_call_target="InvertDiagBlocksLowerTriangular" | custom-call | tf_op jit(solution)/shard_map/triangular_solve | solution.py:20
  420.6 79.4 %custom-call.17 = f32[16,1,64,64]{2,3,1,0:T(8,128)S(1)} custom-call(f32[16,1,64,64]{3,2,1,0:T(8,128)} %get-tuple-element.8), custom_call_target="InvertDiagBlocksLowerTriangular" | custom-call | tf_op jit(solution)/shard_map/triangular_solve | solution.py:16
  500.0 8.0 %convolution_multiply_fusion = f32[16,64,1024]{2,1,0:T(8,128)} fusion(f32[16,64,1024]{2,1,0:T(8,128)} %param.8, f32[16,1,64,64]{2,3,1,0:T(8,128)S(1)} %custom-call.17), kind=kOutput, calls=%fused_computation.3 | convolution fusion | flops 806354944 | bytes 8650752 | tf_op jit(solution)/shard_map/triangular_solve | solution.py:16
  509.7 46.9 %custom-call.28 = f32[8,64,64]{2,1,0:T(8,128)S(1)} custom-call(f32[8,64,64]{2,1,0:T(8,128)S(1)} %fusion.12), custom_call_target="Cholesky" | custom-call | tf_op jit(solution)/shard_map/jit(cholesky)/cholesky | solution.py:45
  556.9 39.3 %custom-call.19 = f32[8,1,64,64]{2,3,1,0:T(8,128)S(1)} custom-call(f32[8,1,64,64]{3,2,1,0:T(8,128)S(1)} %fusion.14), custom_call_target="InvertDiagBlocksLowerTriangular" | custom-call | tf_op jit(solution)/shard_map/triangular_solve | solution.py:20
  597.4 4.9 gather_fusion
  (58 shorter events, 25.6 us)
Async XLA Ops:
  10.8 172.7 %all-to-all-start.1 = ((f32[128,1,2]{2,1,0:T(1,128)}), f32[128,1,2]{2,1,0:T(1,128)S(1)}, u32[]{:S(2)}, u32[]{:S(2)}) async-start(f32[128,1,2]{2,1,0:T(1,128)} %copy.103), calls=%async_computation.1 | async-start | bytes 131072 | tf_op jit(solution)/shard_map/all_to_all | solution.py:70
  29.7 95.9 %copy-start.2 = (s32[128]{0:T(128)S(1)}, s32[128]{0:T(128)}, u32[]{:S(2)}) copy-start(s32[128]{0:T(128)} %param.12) | copy-start | bytes 1540
  183.5 63.1 %all-to-all-start = ((f32[128,2,4096]{2,1,0:T(2,128)}), f32[128,2,4096]{2,1,0:T(2,128)}, u32[]{:S(2)}, u32[]{:S(2)}) async-start(f32[128,2,4096]{2,1,0:T(2,128)} %scatter_fusion), calls=%async_computation | async-start | bytes 8388608 | tf_op jit(solution)/shard_map/all_to_all | solution.py:69
  283.3 5.8 copy-start
  283.3 314.1 %all-to-all-start.2 = ((f32[128,2,4096]{2,1,0:T(2,128)}), f32[128,2,4096]{2,1,0:T(2,128)}, u32[]{:S(2)}, u32[]{:S(2)}) async-start(f32[128,2,4096]{2,1,0:T(2,128)} %reshape.121), calls=%async_computation.2 | async-start | bytes 8388608 | tf_op jit(solution)/shard_map/all_to_all | solution.py:78
  289.2 49.5 %copy-start.1 = (f32[8,4096]{1,0:T(8,128)S(1)}, f32[8,4096]{1,0:T(8,128)}, u32[]{:S(2)}) copy-start(f32[8,4096]{1,0:T(8,128)} %param.10) | copy-start | bytes 393220
  340.2 169.3 %collective-permute-start = (f32[8,64,64]{1,2,0:T(8,128)S(1)}, f32[8,64,64]{1,2,0:T(8,128)S(1)}, u32[]{:S(2)}, u32[]{:S(2)}) collective-permute-start(f32[8,64,64]{1,2,0:T(8,128)S(1)} %fusion.34), channel_id=1, source_target_pairs={{0,32},{32,0},{64,96},{96,64},{1,33},{33,1},{65,97},{97,65},{2,34}... | collective-permute-start | bytes 393224 | tf_op jit(solution)/shard_map/ppermute | solution.py:12
where the time goes:
time: 613 us; the launch traced here: 602 us
  other arithmetic  391 us (64%)
  local copies, waits for them, and re-layouts  88.5 us (14%)
  matrix products  54.5 us (9%)
  waiting for transfers between devices  38 us (6%)
  starting transfers between devices  29.4 us (5%)
    another operation x4, other arithmetic, right_solve(): lax.linalg.triangular_solve(lower, mats, left_side=False, lower=True, tra...  118 us
    another operation x4, other arithmetic, shards(): lower = jnp.linalg.cholesky(gram)  94 us
    another operation x2, other arithmetic, left_solve(): return lax.linalg.triangular_solve(lower, mats, left_side=True, lower=True)  79.4 us
    another operation x3, other arithmetic, shards(): lower_two = jnp.linalg.cholesky(inner_up + partner)  47.1 us
    another operation x3, other arithmetic, shards(): jnp.linalg.cholesky(inner.reshape(leaves // 2, 2, width, width).sum(axis=1))  47.1 us
    all_to_all x1, waiting for transfers between devices, shards(): lax.all_to_all(outgoing, ('grp', 'dev'), split_axis=0, concat_axis=0, til...  38 us
    scatter x1, local copies, waits for them, and re-layouts, shards(): outgoing = jnp.zeros((owners, slots, square), jnp.float32).at[dests, plac...  24.3 us
    dot_general x1, matrix products, shards(): jnp.einsum('bij,bkj->bik', arrived.reshape(sources * count, width, width)...  19.2 us
  transfers between devices with their start and end apart: 4, of which 1 were waited for; matrix products, arithmetic and copies ran while one was open for 80% of the time, Pallas kernels for 0%

commit v1 on v0

v1 whole, which is shorter than its diff:
```python
import functools
import math

import jax
import jax.numpy as jnp
from jax import lax
from jax.experimental import pallas as pl
from jax.experimental.pallas import tpu as pltpu
from jax.sharding import PartitionSpec as P

BOTH = ("grp", "dev")
ROWS = 40
bf16, f32 = jnp.bfloat16, jnp.float32


def cost(flops, moved):
    return pl.CostEstimate(flops=int(flops), bytes_accessed=int(moved), transcendentals=0)


def halves(x):
    high = x.astype(bf16).astype(f32)
    return high, x - high


def left_triple(x):
    high, low = halves(x)
    return jnp.concatenate([high, high, low], axis=1).astype(bf16)


def right_triple(x):
    high, low = halves(x)
    return jnp.concatenate([high, low, high], axis=0).astype(bf16)


def product(first, second):
    return jnp.dot(left_triple(first), right_triple(second), preferred_element_type=f32)


def lanes(shape):
    return lax.broadcasted_iota(jnp.int32, shape, len(shape) - 1)


def sublanes(shape):
    return lax.broadcasted_iota(jnp.int32, shape, len(shape) - 2)


def with_identity(square):
    lane, row = lanes(square.shape), sublanes(square.shape)
    return jnp.where(lane < square.shape[0], square, (lane == row + square.shape[0]).astype(f32))


def eliminate(work, width, batch):
    lane = lanes((batch, 2 * width))
    for j in range(width):
        row = work[j * batch : (j + 1) * batch, :]
        pivot = row[:, j : j + 1]
        if j + 1 < width:
            scaled = row * (1.0 / pivot)
            left = width - 1 - j
            rest = work[(j + 1) * batch :, :].reshape(left, batch, 2 * width)
            rest = rest - rest[:, :, j : j + 1] * scaled[None]
            work[(j + 1) * batch :, :] = rest.reshape(left * batch, 2 * width)
        work[j * batch : (j + 1) * batch, :] = jnp.where(lane >= j, row * lax.rsqrt(pivot), 0.0)


def request_kernel(dest_ref, leaf_ref, tags_ref, place_ref):
    count = dest_ref.shape[1]
    across = jnp.broadcast_to(dest_ref[...].astype(f32), (count, count))
    down = across.T
    first, second = sublanes((count, count)), lanes((count, count))
    earlier = jnp.where((across == down) & (first < second), 1.0, 0.0)
    place = jnp.sum(earlier, axis=0, keepdims=True)
    named = across == first.astype(f32)
    leaf = jnp.broadcast_to(leaf_ref[...].astype(f32), (count, count))
    slot = jnp.broadcast_to(place, (count, count))
    tag_a = jnp.sum(jnp.where(named & (slot == 0.0), leaf, 0.0), axis=1, keepdims=True)
    tag_b = jnp.sum(jnp.where(named & (slot == 1.0), leaf, 0.0), axis=1, keepdims=True)
    tags = jnp.where(second == 0, tag_a, jnp.where(second == 1, tag_b, 0.0))
    tags_ref[...] = tags.astype(jnp.int32)
    place_ref[...] = place.astype(jnp.int32)


def requests(dests, col_leaf):
    count = dests.shape[1]
    return pl.pallas_call(
        request_kernel,
        out_shape=(
            jax.ShapeDtypeStruct((count, count), jnp.int32),
            jax.ShapeDtypeStruct((1, count), jnp.int32),
        ),
        cost_estimate=cost(1e5, 1e5),
        name="requests",
    )(dests, col_leaf)


def factor_kernel(leaves, width, basis_ref, rl_ref, triple_ref, pack_ref, pack_up_ref, work):
    step = pl.program_id(0)
    points = basis_ref.shape[2]
    x = basis_ref[...].reshape(2 * width, points)
    high, low = halves(x)
    both = jnp.concatenate([high, low], axis=0).astype(bf16)
    prod = lax.dot_general(both, both, (((1,), (1,)), ((), ())), preferred_element_type=f32)
    two = 2 * width
    gram = prod[:two, :two] + (prod[:two, two:] + prod[two:, :two]) + prod[two:, two:]
    work[pl.ds(2 * step, width, stride=leaves), :] = with_identity(gram[:width])
    work[pl.ds(2 * step + 1, width, stride=leaves), :] = with_identity(
        pltpu.roll(gram[width:], width, 1)
    )

    @pl.when(step == pl.num_programs(0) - 1)
    def _():
        eliminate(work, width, leaves)
        lane = lanes((two, two))
        half = width // 2
        target = lanes((two, width))
        source = jnp.where(target < half, 2 * target, 2 * (target - half) + 1)
        reorder = (sublanes((two, width)) == source).astype(f32).astype(bf16)
        for b in range(leaves):
            whole = work[pl.ds(b, width, stride=leaves), :]
            rl_ref[b] = whole
            even = work[pl.ds(b, half, stride=2 * leaves), :]
            odd = work[pl.ds(b + leaves, half, stride=2 * leaves), :]
            high, low = halves(jnp.concatenate([even, odd], axis=0))
            both = jnp.concatenate([high, low], axis=0).astype(bf16)
            moved = jnp.dot(both, reorder, preferred_element_type=f32)
            triple_ref[b] = jnp.concatenate(
                [moved[:width], moved[:width], moved[width:]], axis=1
            ).astype(bf16)
            padded = jnp.concatenate([whole, jnp.zeros_like(whole)], axis=0)
            lower = jnp.where(lane < width, padded, 0.0).T[:width]
            pack = jnp.concatenate(
                [
                    lower[48:64],
                    lower[32:48] + pltpu.roll(lower[0:16], 48, 1),
                    lower[16:24] + pltpu.roll(lower[24:32], 32, 1),
                ],
                axis=0,
            )
            pack_ref[b] = pack
            pack_up_ref[b] = pltpu.roll(pack, width, 1)


def leaf_factors(basis):
    leaves, width, points = basis.shape
    whole = lambda *shape: pl.BlockSpec(shape, lambda i: (0,) * len(shape))
    return pl.pallas_call(
        functools.partial(factor_kernel, leaves, width),
        grid=(leaves // 2,),
        in_specs=[pl.BlockSpec((2, width, points), lambda i: (i, 0, 0))],
        out_specs=[
            whole(leaves, width, 2 * width),
            whole(leaves, width, 3 * width),
            whole(leaves, ROWS, 2 * width),
            whole(leaves, ROWS, 2 * width),
        ],
        out_shape=[
            jax.ShapeDtypeStruct((leaves, width, 2 * width), f32),
            jax.ShapeDtypeStruct((leaves, width, 3 * width), bf16),
            jax.ShapeDtypeStruct((leaves, ROWS, 2 * width), f32),
            jax.ShapeDtypeStruct((leaves, ROWS, 2 * width), f32),
        ],
        scratch_shapes=[pltpu.VMEM((width * leaves, 2 * width), f32)],
        cost_estimate=cost(5e9, 6e6),
        name="leaf_factors",
    )(basis)


def reply_kernel(tags_ref, pack_ref, pack_up_ref, out_ref):
    step = pl.program_id(0)
    for r in range(out_ref.shape[0]):
        at = step * out_ref.shape[0] + r
        out_ref[r] = pack_ref[tags_ref[at, 0]] + pack_up_ref[tags_ref[at, 1]]


def replies(tags, pack, pack_up):
    peers = tags.shape[0]
    leaves, rows, wide = pack.shape
    table = pl.BlockSpec((leaves, rows, wide), lambda i: (0, 0, 0))
    return pl.pallas_call(
        reply_kernel,
        grid=(peers // 16,),
        in_specs=[pl.BlockSpec(memory_space=pltpu.SMEM), table, table],
        out_specs=pl.BlockSpec((16, rows, wide), lambda i: (i, 0, 0)),
        out_shape=jax.ShapeDtypeStruct((peers, rows, wide), f32),
        cost_estimate=cost(1e6, 4e6),
        name="replies",
    )(tags, pack, pack_up)


def split_rows(pair):
    width = pair.shape[1] // 2
    return jnp.concatenate([pair[:, :width], pair[:, width:]], axis=0)


def join_rows(square):
    half = square.shape[0] // 2
    return jnp.concatenate([square[:half], square[half:]], axis=1)


def pair_of(ref, n):
    return ref[pl.ds(n // 8 * 256 + n % 8, 32, stride=8), :]


def natural(pair, scratch):
    half, wide = pair.shape
    scratch[pl.ds(0, half, stride=2), :] = pair
    scratch[pl.ds(1, half, stride=2), :] = pltpu.roll(pair, wide // 2, 1)
    return scratch[:, : wide // 2]


def levels_kernel(triple_ref, leaf_ref, upper_ref, lifted_ref, one_ref, two_ref, scratch):
    leaves = triple_ref.shape[0]
    kept = None
    for c in range(leaves // 2):
        upper = natural(pair_of(upper_ref, c), scratch.at[c])
        lifted = []
        for n in (2 * c, 2 * c + 1):
            here = jnp.dot(
                triple_ref[n],
                right_triple(split_rows(pair_of(leaf_ref, n))),
                preferred_element_type=f32,
            )
            lifted_ref[n] = here
            lifted.append(here)
        stack = jnp.concatenate(lifted, axis=0)
        one_ref[c] = product(stack.T, stack)
        image = product(stack, upper)
        second = product(image.T, image)
        if c % 2:
            two_ref[c // 2] = jnp.concatenate([kept, second], axis=1)
        kept = second


def levels(triple, leaf_pairs, upper_pairs):
    leaves, width, _ = triple.shape
    return pl.pallas_call(
        levels_kernel,
        out_shape=[
            jax.ShapeDtypeStruct((leaves, width, width), f32),
            jax.ShapeDtypeStruct((leaves // 2, width, width), f32),
            jax.ShapeDtypeStruct((leaves // 4, width, 2 * width), f32),
        ],
        scratch_shapes=[pltpu.VMEM((leaves // 2, width, 2 * width), f32)],
        cost_estimate=cost(5e9, 2e6),
        name="levels",
    )(triple, leaf_pairs, upper_pairs)


def upper_kernel(one_ref, own_ref, other_ref, lifted_ref, upper_ref, leaf_out, upper_out, work, scratch):
    count, width, _ = one_ref.shape
    batch = 2 * count
    half = width // 2
    for c in range(count):
        one = one_ref[c]
        work[pl.ds(c, width, stride=batch), :] = with_identity(jnp.concatenate([one, one], axis=1))
        summed = own_ref[c // 2] + other_ref[c // 2]
        if c % 2:
            summed = pltpu.roll(summed, width, 1)
        work[pl.ds(count + c, width, stride=batch), :] = with_identity(summed)
    eliminate(work, width, batch)
    for c in range(count):
        inverse = work[pl.ds(c, width, stride=batch), :][:, width:].T
        for n in (2 * c, 2 * c + 1):
            new = product(lifted_ref[n], inverse)
            leaf_out[pl.ds(n // 8 * 256 + n % 8, half, stride=8), :] = join_rows(new)
        even = work[pl.ds(c, half, stride=2 * batch), :][:, :width]
        odd = work[pl.ds(c + batch, half, stride=2 * batch), :][:, :width]
        raised = product(
            jnp.concatenate([even, odd], axis=0), natural(pair_of(upper_ref, c), scratch.at[c])
        )
        inverse = work[pl.ds(count + c, width, stride=batch), :][:, width:].T
        new = product(raised, inverse)
        upper_out[pl.ds(c // 8 * 256 + c % 8, half, stride=8), :] = join_rows(new)


def uppers(one, own, other, lifted, upper_pairs):
    count, width, _ = one.shape
    return pl.pallas_call(
        upper_kernel,
        out_shape=[
            jax.ShapeDtypeStruct((2 * count * width // 2, 2 * width), f32),
            jax.ShapeDtypeStruct((count * width // 2, 2 * width), f32),
        ],
        scratch_shapes=[
            pltpu.VMEM((width * 2 * count, 2 * width), f32),
            pltpu.VMEM((count, width, 2 * width), f32),
        ],
        cost_estimate=cost(5e9, 2e6),
        name="uppers",
    )(one, own, other, lifted, upper_pairs)


def ortho_kernel(factor, rl_ref, basis_ref, out_ref):
    width = basis_ref.shape[1]
    for n in range(basis_ref.shape[0]):
        out_ref[n] = product(rl_ref[n][:, width:] * factor, basis_ref[n])


def ortho(rl, basis):
    leaves, width, points = basis.shape
    return pl.pallas_call(
        functools.partial(ortho_kernel, math.sqrt(points)),
        grid=(leaves // 2,),
        in_specs=[
            pl.BlockSpec((2, width, 2 * width), lambda i: (i, 0, 0)),
            pl.BlockSpec((2, width, points), lambda i: (i, 0, 0)),
        ],
        out_specs=pl.BlockSpec((2, width, points), lambda i: (i, 0, 0)),
        out_shape=jax.ShapeDtypeStruct(basis.shape, f32),
        cost_estimate=cost(5e9, 8e6),
        name="ortho",
    )(rl, basis)


def left_kernel(row_ref, triple_ref, coupling_ref, out_ref):
    step = pl.program_id(0)
    for i in range(8):
        block = split_rows(coupling_ref[pl.ds(i, 32, stride=8), :])
        left = jnp.dot(
            triple_ref[row_ref[0, step * 8 + i]], right_triple(block), preferred_element_type=f32
        )
        out_ref[i] = left_triple(left)


def lefts(row_leaf, triple, coupling_pairs):
    blocks = row_leaf.shape[1]
    leaves, width, _ = triple.shape
    return pl.pallas_call(
        left_kernel,
        grid=(blocks // 8,),
        in_specs=[
            pl.BlockSpec(memory_space=pltpu.SMEM),
            pl.BlockSpec(triple.shape, lambda i: (0, 0, 0)),
            pl.BlockSpec((8 * width // 2, 2 * width), lambda i: (i, 0)),
        ],
        out_specs=pl.BlockSpec((8, width, 3 * width), lambda i: (i, 0, 0)),
        out_shape=jax.ShapeDtypeStruct((blocks, width, 3 * width), bf16),
        cost_estimate=cost(5e9, 6e6),
        name="lefts",
    )(row_leaf, triple, coupling_pairs)


def unpack(pack, place):
    shift = place * 64
    lane = lanes((16, 128))
    first = pltpu.roll(pack[0:16], shift, 1)
    middle = pltpu.roll(pack[16:32], shift, 1)
    corner = pltpu.roll(pack[16:32], lax.rem(shift + 80, 128), 1)
    upper = pltpu.roll(pack[32:40], shift, 1)
    lower = pltpu.roll(pack[32:40], lax.rem(shift + 96, 128), 1)
    narrow = lane[:8] < 32
    return jnp.concatenate(
        [
            jnp.where(lane < 16, corner, 0.0),
            jnp.where(narrow, upper, 0.0),
            jnp.where(narrow, lower, 0.0),
            jnp.where(lane < 48, middle, 0.0),
            first,
        ],
        axis=0,
    )


def finish_kernel(dest_ref, place_ref, left_ref, pack_ref, out_ref):
    step = pl.program_id(0)
    width = left_ref.shape[1]
    for i in range(8):
        at = step * 8 + i
        column = unpack(pack_ref[dest_ref[0, at]], place_ref[0, at])[:, :width]
        done = jnp.dot(left_ref[i], right_triple(column), preferred_element_type=f32)
        out_ref[pl.ds(i, width // 2, stride=8), :] = join_rows(done)


def finish(dests, place, left, packs):
    blocks, width, wide = left.shape
    scalar = pl.BlockSpec(memory_space=pltpu.SMEM)
    return pl.pallas_call(
        finish_kernel,
        grid=(blocks // 8,),
        in_specs=[
            scalar,
            scalar,
            pl.BlockSpec((8, width, wide), lambda i: (i, 0, 0)),
            pl.BlockSpec(packs.shape, lambda i: (0, 0, 0), pipeline_mode=pl.Buffered(1)),
        ],
        out_specs=pl.BlockSpec((8 * width // 2, 2 * width), lambda i: (i, 0)),
        out_shape=jax.ShapeDtypeStruct((blocks * width // 2, 2 * width), f32),
        cost_estimate=cost(5e9, 8e6),
        name="finish",
    )(dests, place, left, packs)


def to_pairs(rows):
    count, square = rows.shape
    tiles = rows.reshape(count // 8, 8, square // 128, 128).transpose(0, 2, 1, 3)
    return tiles.reshape(count * square // 128, 128)


def from_pairs(pairs, square):
    count = pairs.shape[0] * 128 // square
    tiles = pairs.reshape(count // 8, square // 128, 8, 128).transpose(0, 2, 1, 3)
    return tiles.reshape(count, square)


def shards(basis, leaf_transfer, upper_transfer, coupling, row_leaf, col_dev, col_leaf):
    blocks, square = coupling.shape
    dests = col_dev.reshape(1, blocks)
    tags, place = requests(dests, col_leaf.reshape(1, blocks))
    asked = lax.all_to_all(tags, BOTH, split_axis=0, concat_axis=0, tiled=True)
    rl, triple, pack, pack_up = leaf_factors(basis)
    packs = lax.all_to_all(
        replies(asked, pack, pack_up), BOTH, split_axis=0, concat_axis=0, tiled=True
    )
    upper_pairs = to_pairs(upper_transfer)
    lifted, one, own = levels(triple, to_pairs(leaf_transfer), upper_pairs)
    size = lax.axis_size("grp")
    other = lax.ppermute(own, "grp", [(i, i ^ 1) for i in range(size)])
    left = lefts(row_leaf.reshape(1, blocks), triple, to_pairs(coupling))
    ortho_basis = ortho(rl, basis)
    leaf_out, upper_out = uppers(one, own, other, lifted, upper_pairs)
    coupling_out = finish(dests, place, left, packs)
    return (
        ortho_basis,
        from_pairs(leaf_out, square),
        from_pairs(upper_out, square),
        from_pairs(coupling_out, square),
    )


def solution(mesh):
    both = P(BOTH, None)
    in_specs = (P(BOTH, None, None), both, both, both, P(BOTH), both, P(BOTH))
    out_specs = (P(BOTH, None, None), both, both, both)
    return jax.shard_map(shards, mesh=mesh, in_specs=in_specs, out_specs=out_specs, check_vma=False)
```

time: 613 us -> 102 us (0.17); the launches traced: 602 us -> 101 us
  other arithmetic: 391 us -> 0 us
  local copies, waits for them, and re-layouts: 88.5 us -> 2.83 us
  Pallas kernels: 0 us -> 70 us
  matrix products: 54.5 us -> 0 us
  waiting for transfers between devices: 38 us -> 4.78 us
  starting transfers between devices: 29.4 us -> 22.6 us
    another operation x17 -> x0, other arithmetic: 386 us -> none  [the longest x4 118 us: right_solve(): lax.linalg.triangular_solve(lower, mats, left_side=False, lower=True, tra...]
    pallas_call x0 -> x8, Pallas kernels: none -> 70 us  [the longest x1 14.1 us: leaf_factors(): pl.pallas_call(functools.partial(factor_kernel, leaves, width), grid=(lea...]
    dot_general x9 -> x0, matrix products: 45.4 us -> none  [the longest x1 19.2 us: shards(): jnp.einsum('bij,bkj->bik', arrived.reshape(sources * count, width, width)...]
    all_to_all x3 -> x2, waiting for transfers between devices: 38 us -> 0.01 us  [the longest x1 0.01 us: shards(): asked = lax.all_to_all(tags, BOTH, split_axis=0, concat_axis=0, tiled=True)]
    scatter x2 -> x0, local copies, waits for them, and re-layouts: 30.7 us -> none  [the longest x1 24.3 us: shards(): outgoing = jnp.zeros((owners, slots, square), jnp.float32).at[dests, plac...]
    reshape x9 -> x0, local copies, waits for them, and re-layouts: 26.3 us -> none  [the longest x1 8.84 us: shards(): finished.reshape(sources, count, square)]
    dot_general x5 -> x0, local copies, waits for them, and re-layouts: 18.8 us -> none  [the longest x1 9.15 us: shards(): jnp.dot(chosen.reshape(-1, leaves), upper_leaf, precision=exact_mode)]
    another operation x3 -> x0, matrix products: 9.09 us -> none  [the longest x1 8.03 us: left_solve(): return lax.linalg.triangular_solve(lower, mats, left_side=True, lower=True)]
  transfers between devices with their start and end apart: 4 -> 3, of which waited for: 1 -> 1; matrix products, arithmetic and copies ran while one was open for 80% -> 0% of each run, Pallas kernels for 0% -> 49%
where the time goes in v1:
time: 102 us; the launch traced here: 101 us
  Pallas kernels  70 us (69%)
  starting transfers between devices  22.6 us (22%)
  waiting for transfers between devices  4.78 us (5%)
  local copies, waits for them, and re-layouts  2.83 us (3%)
    pallas_call x1, Pallas kernels, leaf_factors(): pl.pallas_call(functools.partial(factor_kernel, leaves, width), grid=(lea...  14.1 us
    pallas_call x1, Pallas kernels, finish(): pl.pallas_call(finish_kernel, grid=(blocks // 8,), in_specs=[scalar, scal...  13.7 us
    pallas_call x1, Pallas kernels, lefts(): pl.pallas_call(left_kernel, grid=(blocks // 8,), in_specs=[pl.BlockSpec(m...  12.9 us
    all_to_all x1, starting transfers between devices, shards(): asked = lax.all_to_all(tags, BOTH, split_axis=0, concat_axis=0, tiled=True)  11.5 us
    all_to_all x1, starting transfers between devices, shards(): lax.all_to_all(replies(asked, pack, pack_up), BOTH, split_axis=0, concat_...  9.74 us
    pallas_call x1, Pallas kernels, uppers(): pl.pallas_call(upper_kernel, out_shape=[jax.ShapeDtypeStruct((2 * count *...  9.5 us
    pallas_call x1, Pallas kernels, ortho(): pl.pallas_call(functools.partial(ortho_kernel, math.sqrt(points)), grid=(...  7.69 us
    pallas_call x1, Pallas kernels, levels(): pl.pallas_call(levels_kernel, out_shape=[jax.ShapeDtypeStruct((leaves, wi...  5.58 us
  transfers between devices with their start and end apart: 3, of which 1 were waited for; matrix products, arithmetic and copies ran while one was open for 0% of the time, Pallas kernels for 49%

profile of v1, /device:TPU:1, one launch (start us, length us, event | category | flops | bytes accessed | tf_op | source)
XLA Modules:
  0.0 100.8 jit_solution(10707398187607775866)
XLA Ops:
  0.6 1.6 %requests.1 = (s32[128,128]{1,0:T(8,128)}, s32[1,128]{1,0:T(1,128)}) custom-call(s32[1,128]{1,0:T(1,128)} %bitcast.45, s32[1,128]{1,0:T(1,128)} %bitcast.43), custom_call_target="tpu_custom_call" | custom-call | flops 100000 | bytes 100000 | tf_op jit(solution)/shard_map/requests/pallas_call | solution.py:85
  2.2 11.5 %all-to-all-start = ((s32[128,1,128]{2,1,0:T(1,128)}), s32[128,1,128]{2,1,0:T(1,128)S(1)}, u32[]{:S(2)}, u32[]{:S(2)}) async-start(s32[128,1,128]{2,1,0:T(1,128)} %bitcast.38), calls=%async_computation | async-start | bytes 131072 | tf_op jit(solution)/shard_map/all_to_all | solution.py:409
  13.7 14.1 %leaf_factors.1 = (f32[16,64,128]{2,1,0:T(8,128)}, bf16[16,64,192]{2,1,0:T(8,128)(2,1)}, f32[16,40,128]{2,1,0:T(8,128)}, f32[16,40,128]{2,1,0:T(8,128)}) custom-call(f32[16,64,1024]{2,1,0:T(8,128)} %basis_ref.3), custom_call_target="tpu_custom_call" | custom-call | flops 5000000000 | bytes 6000000 | tf_op jit(solution)/shard_map/leaf_factors/pallas_call | solution.py:146
  27.8 0.0 all-to-all-done
  27.8 0.0 copy-start.1
  27.8 0.6 copy-done.1
  28.4 5.0 %replies.1 = f32[128,40,128]{2,1,0:T(8,128)} custom-call(s32[128,128]{1,0:T(8,128)} %bitcast.37, f32[16,40,128]{2,1,0:T(8,128)} %get-tuple-element.24.pack_ref, f32[16,40,128]{2,1,0:T(8,128)} %get-tuple-element.25.pack_up_ref), custom_call_target="tpu_custom_call" | custom-call | flops 1000000 | bytes 4000000 | tf_op jit(solution)/shard_map/replies/pallas_call | solution.py:179
  33.4 9.7 %all-to-all-start.1 = ((f32[128,40,128]{2,1,0:T(8,128)}), f32[128,40,128]{2,1,0:T(8,128)S(1)}, u32[]{:S(2)}, u32[]{:S(2)}) async-start(f32[128,40,128]{2,1,0:T(8,128)} %replies.1), calls=%async_computation.1 | async-start | bytes 5242880 | tf_op jit(solution)/shard_map/all_to_all | solution.py:411
  43.2 5.6 %levels.1 = (f32[16,64,64]{2,1,0:T(8,128)}, f32[8,64,64]{2,1,0:T(8,128)}, f32[4,64,128]{2,1,0:T(8,128)}) custom-call(bf16[16,64,192]{2,1,0:T(8,128)(2,1)} %get-tuple-element.16.triple_ref, f32[512,128]{1,0:T(8,128)} %bitcast.40, f32[256,128]{1,0:T(8,128)} %bitcast.41), custom_call_target="tpu_custom_call" | custom-call | flops 5000000000 | bytes 2000000 | tf_op jit(solution)/shard_map/levels/pallas_call | solution.py:236
  48.7 1.4 %collective-permute-start = (f32[4,64,128]{2,1,0:T(8,128)}, f32[4,64,128]{2,1,0:T(8,128)S(1)}, u32[]{:S(2)}, u32[]{:S(2)}) collective-permute-start(f32[4,64,128]{2,1,0:T(8,128)} %get-tuple-element.18.own_ref), channel_id=1, source_target_pairs={{0,32},{32,0},{64,96},{96,64},{1,33},{33,1},{65,97},{97,65},{2,34}... | collective-permute-start | bytes 393224 | tf_op jit(solution)/shard_map/ppermute | solution.py:417
  50.1 7.7 %ortho.1 = f32[16,64,1024]{2,1,0:T(8,128)} custom-call(f32[16,64,128]{2,1,0:T(8,128)} %get-tuple-element.15.rl_ref, f32[16,64,1024]{2,1,0:T(8,128)} %basis_ref.3), custom_call_target="tpu_custom_call" | custom-call | flops 5000000000 | bytes 8000000 | tf_op jit(solution)/shard_map/ortho/pallas_call | solution.py:301
  57.8 12.9 %lefts.1.left_ref = bf16[128,64,192]{2,1,0:T(8,128)(2,1)} custom-call(s32[1,128]{1,0:T(1,128)} %bitcast.44, bf16[16,64,192]{2,1,0:T(8,128)(2,1)} %get-tuple-element.16.triple_ref, f32[4096,128]{1,0:T(8,128)} %bitcast.39), custom_call_target="tpu_custom_call" | custom-call | flops 5000000000 | bytes 6000000 | tf_op jit(solution)/shard_map/lefts/pallas_call | solution.py:328
  70.6 4.8 %collective-permute-done.other_ref = f32[4,64,128]{2,1,0:T(8,128)S(1)} collective-permute-done((f32[4,64,128]{2,1,0:T(8,128)}, f32[4,64,128]{2,1,0:T(8,128)S(1)}, u32[]{:S(2)}, u32[]{:S(2)}) %collective-permute-start) | collective-permute-done | bytes 131104 | tf_op jit(solution)/shard_map/ppermute | solution.py:417
  75.4 0.0 copy-start.2
  75.4 0.7 copy-done.2
  76.1 9.5 %uppers.1 = (f32[512,128]{1,0:T(8,128)}, f32[256,128]{1,0:T(8,128)}) custom-call(f32[8,64,64]{2,1,0:T(8,128)} %get-tuple-element.17.one_ref, f32[4,64,128]{2,1,0:T(8,128)} %get-tuple-element.18.own_ref, f32[4,64,128]{2,1,0:T(8,128)} %copy-done.2, f32[16,64,64]{2,1,0:T(8,128)} %get-tuple-element.19.lifted_ref, f32[256,128]{1,0:T(8,128)} %bitcast.42), custom_call_target="tpu_custom_call" | custom-call | flops 5000000000 | bytes 2000000 | tf_op jit(solution)/shard_map/uppers/pallas_call | solution.py:278
  85.6 0.0 all-to-all-done.1.pack_ref
  85.6 0.0 copy-start
  85.6 1.5 %copy-done = f32[128,40,128]{2,1,0:T(8,128)} copy-done((f32[128,40,128]{2,1,0:T(8,128)}, f32[128,40,128]{2,1,0:T(8,128)S(1)}, u32[]{:S(2)}) %copy-start) | copy-done | bytes 2621464
  87.1 13.7 %finish.1 = f32[4096,128]{1,0:T(8,128)} custom-call(s32[1,128]{1,0:T(1,128)} %bitcast.46, s32[1,128]{1,0:T(1,128)} %get-tuple-element.22.place_ref, bf16[128,64,192]{2,1,0:T(8,128)(2,1)} %lefts.1.left_ref, f32[128,40,128]{2,1,0:T(8,128)} %copy-done), custom_call_target="tpu_custom_call" | custom-call | flops 5000000000 | bytes 8000000 | tf_op jit(solution)/shard_map/finish/pallas_call | solution.py:377
Async XLA Ops:
  2.2 25.6 %all-to-all-start = ((s32[128,1,128]{2,1,0:T(1,128)}), s32[128,1,128]{2,1,0:T(1,128)S(1)}, u32[]{:S(2)}, u32[]{:S(2)}) async-start(s32[128,1,128]{2,1,0:T(1,128)} %bitcast.38), calls=%async_computation | async-start | bytes 131072 | tf_op jit(solution)/shard_map/all_to_all | solution.py:409
  27.8 0.6 copy-start.1
  33.4 52.2 %all-to-all-start.1 = ((f32[128,40,128]{2,1,0:T(8,128)}), f32[128,40,128]{2,1,0:T(8,128)S(1)}, u32[]{:S(2)}, u32[]{:S(2)}) async-start(f32[128,40,128]{2,1,0:T(8,128)} %replies.1), calls=%async_computation.1 | async-start | bytes 5242880 | tf_op jit(solution)/shard_map/all_to_all | solution.py:411
  48.7 26.7 %collective-permute-start = (f32[4,64,128]{2,1,0:T(8,128)}, f32[4,64,128]{2,1,0:T(8,128)S(1)}, u32[]{:S(2)}, u32[]{:S(2)}) collective-permute-start(f32[4,64,128]{2,1,0:T(8,128)} %get-tuple-element.18.own_ref), channel_id=1, source_target_pairs={{0,32},{32,0},{64,96},{96,64},{1,33},{33,1},{65,97},{97,65},{2,34}... | collective-permute-start | bytes 393224 | tf_op jit(solution)/shard_map/ppermute | solution.py:417
  75.4 0.7 copy-start.2
  85.6 1.5 %copy-start = (f32[128,40,128]{2,1,0:T(8,128)}, f32[128,40,128]{2,1,0:T(8,128)S(1)}, u32[]{:S(2)}) copy-start(f32[128,40,128]{2,1,0:T(8,128)S(1)} %all-to-all-done.1.pack_ref) | copy-start | bytes 7864324

commit v2 on v1

v2 whole, which is shorter than its diff:
```python
import functools
import math

import jax
import jax.numpy as jnp
from jax import lax
from jax.experimental import pallas as pl
from jax.experimental.pallas import tpu as pltpu
from jax.sharding import PartitionSpec as P

BOTH = ("grp", "dev")
ROWS = 36
ROOM = pltpu.CompilerParams(vmem_limit_bytes=24 << 20)
VMEM = pl.BlockSpec(memory_space=pltpu.VMEM)
HBM = pl.BlockSpec(memory_space=pltpu.HBM)
bf16, f32 = jnp.bfloat16, jnp.float32


def cost(flops, moved):
    return pl.CostEstimate(flops=int(flops), bytes_accessed=int(moved), transcendentals=0)


def halves(x):
    high = x.astype(bf16).astype(f32)
    return high, x - high


def left_triple(x):
    high, low = halves(x)
    return jnp.concatenate([high, high, low], axis=1).astype(bf16)


def right_triple(x):
    high, low = halves(x)
    return jnp.concatenate([high, low, high], axis=0).astype(bf16)


def product(first, second):
    return jnp.dot(left_triple(first), right_triple(second), preferred_element_type=f32)


def lanes(shape):
    return lax.broadcasted_iota(jnp.int32, shape, len(shape) - 1)


def sublanes(shape):
    return lax.broadcasted_iota(jnp.int32, shape, len(shape) - 2)


def with_identity(square):
    lane, row = lanes(square.shape), sublanes(square.shape)
    return jnp.where(lane < square.shape[0], square, (lane == row + square.shape[0]).astype(f32))


def eliminate(work, width, batch):
    wide = 2 * width
    lane = lanes((batch, wide))

    def store(i, value):
        work[i * batch : (i + 1) * batch, :] = jnp.where(lane >= i, value, 0.0)

    for j in range(0, width, 4):
        r0, r1, r2, r3 = [work[(j + k) * batch : (j + k + 1) * batch, :] for k in range(4)]
        at = lambda row, k: jnp.broadcast_to(row[:, j + k : j + k + 1], (batch, wide))
        a, b, c = at(r0, 0), at(r0, 1), at(r1, 1)
        p02, p03, p12, p13 = at(r0, 2), at(r0, 3), at(r1, 2), at(r1, 3)
        det = a * c - b * b
        inv = 1.0 / det
        x00, x10 = (c * p02 - b * p12) * inv, (a * p12 - b * p02) * inv
        x01, x11 = (c * p03 - b * p13) * inv, (a * p13 - b * p03) * inv
        s00 = at(r2, 2) - (p02 * x00 + p12 * x10)
        s01 = at(r2, 3) - (p02 * x01 + p12 * x11)
        s11 = at(r3, 3) - (p03 * x01 + p13 * x11)
        det_s = s00 * s11 - s01 * s01
        inv_s = 1.0 / det_s
        q2 = r2 - x00 * r0 - x10 * r1
        q3 = r3 - x01 * r0 - x11 * r1
        n1 = a * r1 - b * r0
        n3 = s00 * q3 - s01 * q2
        left = width - 4 - j
        if left:
            w0, w1 = (s11 * q2 - s01 * q3) * inv_s, n3 * inv_s
            v0 = (c * r0 - b * r1) * inv - x00 * w0 - x01 * w1
            v1 = n1 * inv - x10 * w0 - x11 * w1
            rest = work[(j + 4) * batch :, :].reshape(left, batch, wide)
            col = lambda k: rest[:, :, j + k : j + k + 1]
            rest = rest - ((col(0) * v0 + col(1) * v1) + (col(2) * w0 + col(3) * w1))
            work[(j + 4) * batch :, :] = rest.reshape(left * batch, wide)
        ra, rs = lax.rsqrt(a), lax.rsqrt(s00)
        store(j, r0 * ra)
        store(j + 1, n1 * (ra * lax.rsqrt(det)))
        store(j + 2, q2 * rs)
        store(j + 3, n3 * (rs * lax.rsqrt(det_s)))


def eliminate_small(work, width, batch):
    wide = 2 * width
    lane = lanes((batch, wide))
    rows = [work[i * batch : (i + 1) * batch, :] for i in range(width)]
    at = lambda row, k: jnp.broadcast_to(row[:, k : k + 1], (batch, wide))

    def store(i, value):
        work[i * batch : (i + 1) * batch, :] = jnp.where(lane >= i, value, 0.0)

    for j in range(0, width, 2):
        r0, r1 = rows[j], rows[j + 1]
        a, b, c = at(r0, j), at(r0, j + 1), at(r1, j + 1)
        det = a * c - b * b
        inv = 1.0 / det
        n0, n1 = c * r0 - b * r1, a * r1 - b * r0
        for i in range(j + 2, width):
            rows[i] = rows[i] - (at(rows[i], j) * n0 + at(rows[i], j + 1) * n1) * inv
        ra = lax.rsqrt(a)
        store(j, r0 * ra)
        store(j + 1, n1 * (ra * lax.rsqrt(det)))


def request_kernel(dest_ref, leaf_ref, tags_ref, place_ref):
    count = dest_ref.shape[1]
    across = jnp.broadcast_to(dest_ref[...].astype(f32), (count, count))
    down = across.T
    first, second = sublanes((count, count)), lanes((count, count))
    earlier = jnp.where((across == down) & (first < second), 1.0, 0.0)
    place = jnp.sum(earlier, axis=0, keepdims=True)
    named = across == first.astype(f32)
    leaf = jnp.broadcast_to(leaf_ref[...].astype(f32), (count, count))
    slot = jnp.broadcast_to(place, (count, count))
    tag_a = jnp.sum(jnp.where(named & (slot == 0.0), leaf, 0.0), axis=1, keepdims=True)
    tag_b = jnp.sum(jnp.where(named & (slot == 1.0), leaf, 0.0), axis=1, keepdims=True)
    tags = jnp.where(second == 0, tag_a, jnp.where(second == 1, tag_b, 0.0))
    tags_ref[...] = tags.astype(jnp.int32)
    place_ref[...] = place.astype(jnp.int32)


def requests(dests, col_leaf):
    count = dests.shape[1]
    return pl.pallas_call(
        request_kernel,
        out_shape=(
            jax.ShapeDtypeStruct((count, count), jnp.int32),
            jax.ShapeDtypeStruct((1, count), jnp.int32),
        ),
        cost_estimate=cost(1e5, 1e5),
        name="requests",
    )(dests, col_leaf)


def pack_rows(lower):
    moved = lambda start, stop, lane: pltpu.roll(lower[start:stop], lane, 1)
    quarter = lower[24:32]
    last = quarter + pltpu.roll(pltpu.roll(quarter, 4, 0), 32, 1)
    return jnp.concatenate(
        [
            lower[56:64],
            lower[48:56] + moved(0, 8, 56),
            lower[40:48] + moved(8, 16, 48),
            lower[32:40] + moved(16, 24, 40),
            jnp.where(sublanes(last.shape) < 4, last, 0.0),
        ],
        axis=0,
    )


def factor_kernel(
    leaves, width, source_ref, rl_ref, triple_ref, pack_ref, pack_up_ref, work, basis_ref, sems
):
    count, _, points = basis_ref.shape
    pieces = sems.shape[0]
    size = count // pieces
    copies = [
        pltpu.make_async_copy(
            source_ref.at[pl.ds(p * size, size)], basis_ref.at[pl.ds(p * size, size)], sems.at[p]
        )
        for p in range(pieces)
    ]
    for copy in copies:
        copy.start()
    two = 2 * width
    for q in range(0, count, 2):
        if q % size == 0:
            copies[q // size].wait()
        high, low = halves(basis_ref[q : q + 2].reshape(two, points))
        both = jnp.concatenate([high, low], axis=0).astype(bf16)
        prod = lax.dot_general(both, both, (((1,), (1,)), ((), ())), preferred_element_type=f32)
        gram = prod[:two, :two] + (prod[:two, two:] + prod[two:, :two]) + prod[two:, two:]
        work[pl.ds(q, width, stride=leaves), :] = with_identity(gram[:width])
        work[pl.ds(q + 1, width, stride=leaves), :] = with_identity(
            pltpu.roll(gram[width:], width, 1)
        )

    eliminate(work, width, leaves)
    lane = lanes((two, two))
    half = width // 2
    target = lanes((two, width))
    source = jnp.where(target < half, 2 * target, 2 * (target - half) + 1)
    reorder = (sublanes((two, width)) == source).astype(f32).astype(bf16)
    for b in range(leaves):
        whole = work[pl.ds(b, width, stride=leaves), :]
        rl_ref[b] = whole
        even = work[pl.ds(b, half, stride=2 * leaves), :]
        odd = work[pl.ds(b + leaves, half, stride=2 * leaves), :]
        high, low = halves(jnp.concatenate([even, odd], axis=0))
        both = jnp.concatenate([high, low], axis=0).astype(bf16)
        moved = jnp.dot(both, reorder, preferred_element_type=f32)
        triple_ref[b] = jnp.concatenate(
            [moved[:width], moved[:width], moved[width:]], axis=1
        ).astype(bf16)
        padded = jnp.concatenate([whole, jnp.zeros_like(whole)], axis=0)
        lower = jnp.where(lane < width, padded, 0.0).T[:width]
        pack = pack_rows(lower)
        pack_ref[b] = pack
        pack_up_ref[b] = pltpu.roll(pack, width, 1)


def leaf_factors(basis):
    leaves, width, points = basis.shape
    return pl.pallas_call(
        functools.partial(factor_kernel, leaves, width),
        in_specs=[HBM],
        out_specs=[VMEM] * 4,
        out_shape=[
            jax.ShapeDtypeStruct((leaves, width, 2 * width), f32),
            jax.ShapeDtypeStruct((leaves, width, 3 * width), bf16),
            jax.ShapeDtypeStruct((leaves, 40, 2 * width), f32),
            jax.ShapeDtypeStruct((leaves, 40, 2 * width), f32),
        ],
        scratch_shapes=[
            pltpu.VMEM((width * leaves, 2 * width), f32),
            pltpu.VMEM(basis.shape, f32),
            pltpu.SemaphoreType.DMA((leaves // 4,)),
        ],
        compiler_params=pltpu.CompilerParams(vmem_limit_bytes=53248 << 10),
        cost_estimate=cost(5e9, 6e6),
        name="leaf_factors",
    )(basis)


def reply_kernel(tags_ref, pack_ref, pack_up_ref, out_ref, line, table, sem):
    step = pl.program_id(0)
    count = out_ref.shape[0] // ROWS

    @pl.when(step == 0)
    def _():
        line[...] = tags_ref[...].astype(f32).T[:8].astype(jnp.int32)
        copy = pltpu.make_async_copy(line, table, sem)
        copy.start()
        copy.wait()

    for r in range(0, count, 2):
        at = step * count + r
        even = pack_ref[table[0, at]] + pack_up_ref[table[1, at]]
        odd = pack_ref[table[0, at + 1]] + pack_up_ref[table[1, at + 1]]
        odd = pltpu.roll(odd, 4, 0)
        out_ref[r * ROWS : r * ROWS + 32] = even[:32]
        out_ref[r * ROWS + 32 : r * ROWS + 40] = even[32:] + odd[:8]
        out_ref[r * ROWS + 40 : (r + 2) * ROWS] = odd[8:]


def replies(tags, pack, pack_up):
    peers = tags.shape[0]
    leaves, rows, wide = pack.shape
    table = pl.BlockSpec((leaves, rows, wide), lambda i: (0, 0, 0))
    per = peers // 2
    return pl.pallas_call(
        reply_kernel,
        grid=(peers // per,),
        in_specs=[pl.BlockSpec(tags.shape, lambda i: (0, 0)), table, table],
        out_specs=pl.BlockSpec((per * ROWS, wide), lambda i: (i, 0)),
        out_shape=jax.ShapeDtypeStruct((peers * ROWS, wide), f32),
        scratch_shapes=[
            pltpu.VMEM((8, peers), jnp.int32),
            pltpu.SMEM((8, peers), jnp.int32),
            pltpu.SemaphoreType.DMA,
        ],
        compiler_params=ROOM,
        cost_estimate=cost(1e6, 4e6),
        name="replies",
    )(tags, pack, pack_up)


def split_rows(pair):
    width = pair.shape[1] // 2
    return jnp.concatenate([pair[:, :width], pair[:, width:]], axis=0)


def join_rows(square):
    half = square.shape[0] // 2
    return jnp.concatenate([square[:half], square[half:]], axis=1)


def pair_of(ref, n):
    return ref[pl.ds(n // 8 * 256 + n % 8, 32, stride=8), :]


def natural(pair, scratch):
    half, wide = pair.shape
    scratch[pl.ds(0, half, stride=2), :] = pair
    scratch[pl.ds(1, half, stride=2), :] = pltpu.roll(pair, wide // 2, 1)
    return scratch[:, : wide // 2]


def levels_kernel(triple_ref, leaf_ref, upper_ref, lifted_ref, one_ref, two_ref, scratch):
    leaves = triple_ref.shape[0]
    kept = None
    for c in range(leaves // 2):
        upper = natural(pair_of(upper_ref, c), scratch.at[c])
        lifted = []
        for n in (2 * c, 2 * c + 1):
            here = jnp.dot(
                triple_ref[n],
                right_triple(split_rows(pair_of(leaf_ref, n))),
                preferred_element_type=f32,
            )
            lifted_ref[n] = here
            lifted.append(here)
        stack = jnp.concatenate(lifted, axis=0)
        one_ref[c] = product(stack.T, stack)
        image = product(stack, upper)
        second = product(image.T, image)
        if c % 2:
            two_ref[c // 2] = jnp.concatenate([kept, second], axis=1)
        kept = second


def levels(triple, leaf_pairs, upper_pairs):
    leaves, width, _ = triple.shape
    return pl.pallas_call(
        levels_kernel,
        out_shape=[
            jax.ShapeDtypeStruct((leaves, width, width), f32),
            jax.ShapeDtypeStruct((leaves // 2, width, width), f32),
            jax.ShapeDtypeStruct((leaves // 4, width, 2 * width), f32),
        ],
        scratch_shapes=[pltpu.VMEM((leaves // 2, width, 2 * width), f32)],
        compiler_params=ROOM,
        cost_estimate=cost(5e9, 2e6),
        name="levels",
    )(triple, leaf_pairs, upper_pairs)


def one_kernel(one_ref, lifted_ref, upper_ref, leaf_out, raised_out, work, scratch):
    count, width, _ = one_ref.shape
    half = width // 2
    for c in range(count):
        one = one_ref[c]
        work[pl.ds(c, width, stride=count), :] = with_identity(jnp.concatenate([one, one], axis=1))
    eliminate_small(work, width, count)
    for c in range(count):
        inverse = work[pl.ds(c, width, stride=count), :][:, width:].T
        for n in (2 * c, 2 * c + 1):
            new = product(lifted_ref[n], inverse)
            leaf_out[pl.ds(n // 8 * 256 + n % 8, half, stride=8), :] = join_rows(new)
        even = work[pl.ds(c, half, stride=2 * count), :][:, :width]
        odd = work[pl.ds(c + count, half, stride=2 * count), :][:, :width]
        raised_out[c] = product(
            jnp.concatenate([even, odd], axis=0), natural(pair_of(upper_ref, c), scratch.at[c])
        )


def level_one(one, lifted, upper_pairs):
    count, width, _ = one.shape
    return pl.pallas_call(
        one_kernel,
        in_specs=[VMEM] * 3,
        out_specs=[VMEM] * 2,
        out_shape=[
            jax.ShapeDtypeStruct((count * width, 2 * width), f32),
            jax.ShapeDtypeStruct((count, width, width), f32),
        ],
        scratch_shapes=[
            pltpu.VMEM((width * count, 2 * width), f32),
            pltpu.VMEM((count, width, 2 * width), f32),
        ],
        compiler_params=ROOM,
        cost_estimate=cost(3e9, 2e6),
        name="level_one",
    )(one, lifted, upper_pairs)


def two_kernel(own_ref, other_ref, raised_ref, upper_out, work):
    count, width, _ = raised_ref.shape
    for c in range(count):
        summed = own_ref[c // 2] + other_ref[c // 2]
        if c % 2:
            summed = pltpu.roll(summed, width, 1)
        work[pl.ds(c, width, stride=count), :] = with_identity(summed)
    eliminate_small(work, width, count)
    for c in range(count):
        inverse = work[pl.ds(c, width, stride=count), :][:, width:].T
        new = product(raised_ref[c], inverse)
        upper_out[pl.ds(c // 8 * 256 + c % 8, width // 2, stride=8), :] = join_rows(new)


def level_two(own, other, raised):
    count, width, _ = raised.shape
    return pl.pallas_call(
        two_kernel,
        in_specs=[VMEM] * 3,
        out_specs=VMEM,
        out_shape=jax.ShapeDtypeStruct((count * width // 2, 2 * width), f32),
        scratch_shapes=[pltpu.VMEM((width * count, 2 * width), f32)],
        compiler_params=ROOM,
        cost_estimate=cost(1e9, 1e6),
        name="level_two",
    )(own, other, raised)


def ortho_kernel(factor, rl_ref, basis_ref, out_ref):
    width = basis_ref.shape[1]
    for n in range(basis_ref.shape[0]):
        out_ref[n] = product(rl_ref[n][:, width:] * factor, basis_ref[n])


def ortho(rl, basis):
    leaves, width, points = basis.shape
    return pl.pallas_call(
        functools.partial(ortho_kernel, math.sqrt(points)),
        grid=(2,),
        in_specs=[
            pl.BlockSpec((leaves // 2, width, 2 * width), lambda i: (i, 0, 0)),
            pl.BlockSpec((leaves // 2, width, points), lambda i: (i, 0, 0)),
        ],
        out_specs=pl.BlockSpec((leaves // 2, width, points), lambda i: (i, 0, 0)),
        out_shape=jax.ShapeDtypeStruct(basis.shape, f32),
        compiler_params=ROOM,
        cost_estimate=cost(5e9, 8e6),
        name="ortho",
    )(rl, basis)


def left_kernel(row_ref, triple_ref, coupling_ref, out_ref):
    step = pl.program_id(0)
    count = 2 * out_ref.shape[0]

    def group(g, _):
        for q in range(16):
            at = g * 32 + 2 * q
            pair = []
            for i in range(2):
                block = coupling_ref[pl.ds(g * 1024 + q // 4 * 256 + (2 * q + i) % 8, 32, stride=8), :]
                pair.append(
                    jnp.dot(
                        triple_ref[row_ref[0, step * count + at + i]],
                        right_triple(split_rows(block)),
                        preferred_element_type=f32,
                    )
                )
            high, low = halves(jnp.concatenate(pair, axis=1))
            out_ref[g * 16 + q] = jnp.concatenate([high, low], axis=0).astype(bf16)
        return 0

    lax.fori_loop(0, count // 32, group, 0)


def lefts(row_leaf, triple, coupling_pairs):
    blocks = row_leaf.shape[1]
    leaves, width, _ = triple.shape
    wide = 2 * width
    per = blocks // 2
    return pl.pallas_call(
        left_kernel,
        grid=(blocks // per,),
        in_specs=[
            pl.BlockSpec(memory_space=pltpu.SMEM),
            pl.BlockSpec(triple.shape, lambda i: (0, 0, 0)),
            pl.BlockSpec((per * width // 2, wide), lambda i: (i, 0)),
        ],
        out_specs=pl.BlockSpec((per // 2, wide, wide), lambda i: (i, 0, 0)),
        out_shape=jax.ShapeDtypeStruct((blocks // 2, wide, wide), bf16),
        compiler_params=ROOM,
        cost_estimate=cost(5e9, 6e6),
        name="lefts",
    )(row_leaf, triple, coupling_pairs)


def unpack(ref, base, place, side):
    lane = lanes((8, 128)) - 64 * side
    shift = (place ^ side) * 64

    def piece(rows, start, count):
        turned = pltpu.roll(rows, lax.rem(shift + (128 - start), 128), 1)
        return jnp.where((lane >= 0) & (lane < count), turned, 0.0)

    first, second, third, fourth = [ref[pl.ds(base + 8 * k, 8), :] for k in range(4)]
    last = ref[pl.ds(base + 28, 8), :]
    middle = jnp.where(
        sublanes((8, 128)) < 4,
        pltpu.roll(piece(last, 0, 32), 4, 0),
        piece(last, 32, 32),
    )
    return jnp.concatenate(
        [
            piece(second, 56, 8),
            piece(third, 48, 16),
            piece(fourth, 40, 24),
            middle,
            piece(fourth, 0, 40),
            piece(third, 0, 48),
            piece(second, 0, 56),
            piece(first, 0, 64),
        ],
        axis=0,
    )


def finish_kernel(
    dest_ref, place_ref, left_hbm, pack_ref, out_hbm, left_ref, out_ref, in_sems, out_sems
):
    pairs, wide, _ = left_ref.shape
    width = wide // 2
    lane = lanes((width // 2, wide))
    groups = in_sems.shape[0]
    size = pairs // groups
    rows = size * wide // 2

    def fetch(g):
        part = pl.ds(g * size, size)
        return pltpu.make_async_copy(left_hbm.at[part], left_ref.at[part], in_sems.at[g])

    def put(g):
        part = pl.ds(pl.multiple_of(g * rows, rows), rows)
        return pltpu.make_async_copy(out_ref.at[part], out_hbm.at[part], out_sems.at[g])

    for g in range(groups):
        fetch(g).start()

    def group(g, _):
        fetch(g).wait()
        for q in range(size):
            lower = []
            for i in range(2):
                at = (g * size + q) * 2 + i
                lower.append(unpack(pack_ref, dest_ref[0, at] * ROWS, place_ref[0, at], i))
            high, low = halves(jnp.concatenate(lower, axis=0))
            left = left_ref[g * size + q]
            both = jnp.dot(left, high.astype(bf16), preferred_element_type=f32)
            done = (
                both[:width]
                + both[width:]
                + jnp.dot(left[:width], low.astype(bf16), preferred_element_type=f32)
            )
            even, odd = done[: width // 2], done[width // 2 :]
            base = g * rows + q // 4 * 256 + 2 * q % 8
            out_ref[pl.ds(base, 32, stride=8), :] = jnp.where(
                lane < width, even, pltpu.roll(odd, width, 1)
            )
            out_ref[pl.ds(base + 1, 32, stride=8), :] = jnp.where(
                lane < width, pltpu.roll(even, width, 1), odd
            )
        put(g).start()
        return 0

    lax.fori_loop(0, groups, group, 0)
    for g in range(groups):
        put(g).wait()


def finish(dests, place, left, packs):
    pairs, wide, _ = left.shape
    scalar = pl.BlockSpec(memory_space=pltpu.SMEM)
    shape = (pairs * wide // 2, wide)
    return pl.pallas_call(
        finish_kernel,
        in_specs=[scalar, scalar, HBM, VMEM],
        out_specs=HBM,
        out_shape=jax.ShapeDtypeStruct(shape, f32),
        scratch_shapes=[
            pltpu.VMEM(left.shape, bf16),
            pltpu.VMEM(shape, f32),
            pltpu.SemaphoreType.DMA((4,)),
            pltpu.SemaphoreType.DMA((4,)),
        ],
        compiler_params=pltpu.CompilerParams(vmem_limit_bytes=53248 << 10),
        cost_estimate=cost(5e9, 8e6),
        name="finish",
    )(dests, place, left, packs)


def to_pairs(rows):
    count, square = rows.shape
    tiles = rows.reshape(count // 8, 8, square // 128, 128).transpose(0, 2, 1, 3)
    return tiles.reshape(count * square // 128, 128)


def from_pairs(pairs, square):
    count = pairs.shape[0] * 128 // square
    tiles = pairs.reshape(count // 8, square // 128, 8, 128).transpose(0, 2, 1, 3)
    return tiles.reshape(count, square)


def shards(basis, leaf_transfer, upper_transfer, coupling, row_leaf, col_dev, col_leaf):
    blocks, square = coupling.shape
    dests = col_dev.reshape(1, blocks)
    tags, place = requests(dests, col_leaf.reshape(1, blocks))
    asked = lax.all_to_all(tags, BOTH, split_axis=0, concat_axis=0, tiled=True)
    rl, triple, pack, pack_up = leaf_factors(basis)
    answers = replies(asked, pack, pack_up).reshape(asked.shape[0], 1, -1)
    packs = lax.all_to_all(answers, BOTH, split_axis=0, concat_axis=0, tiled=True)
    packs = packs.reshape(-1, pack.shape[2])
    upper_pairs = to_pairs(upper_transfer)
    lifted, one, own = levels(triple, to_pairs(leaf_transfer), upper_pairs)
    size = lax.axis_size("grp")
    other = lax.ppermute(own, "grp", [(i, i ^ 1) for i in range(size)])
    left = lefts(row_leaf.reshape(1, blocks), triple, to_pairs(coupling))
    ortho_basis = ortho(rl, basis)
    leaf_out, raised = level_one(one, lifted, upper_pairs)
    upper_out = level_two(own, other, raised)
    coupling_out = finish(dests, place, left, packs)
    return (
        ortho_basis,
        from_pairs(leaf_out, square),
        from_pairs(upper_out, square),
        from_pairs(coupling_out, square),
    )


def solution(mesh):
    both = P(BOTH, None)
    in_specs = (P(BOTH, None, None), both, both, both, P(BOTH), both, P(BOTH))
    out_specs = (P(BOTH, None, None), both, both, both)
    return jax.shard_map(shards, mesh=mesh, in_specs=in_specs, out_specs=out_specs, check_vma=False)
```

time: 102 us -> 76.6 us (0.75)
  Pallas kernels: 70 us -> 39.3 us
  waiting for transfers between devices: 4.78 us -> 12.8 us
  local copies, waits for them, and re-layouts: 2.83 us -> 0.04 us
    pallas_call x5 -> x6, Pallas kernels: 55.1 us -> 31.2 us  [the longest x1 9.73 us: leaf_factors(): pl.pallas_call(functools.partial(factor_kernel, leaves, width), in_specs=...]
    ppermute x1, waiting for transfers between devices: 4.77 us -> 12.8 us  [shards(): other = lax.ppermute(own, 'grp', [(i, i ^ 1) for i in range(size)])]
    pallas_call x1, Pallas kernels: 7.69 us -> 2.86 us  [ortho(): pl.pallas_call(functools.partial(ortho_kernel, math.sqrt(points)), grid=(...]
    unnamed x6 -> x16, local copies, waits for them, and re-layouts: 2.83 us -> 0.04 us
    pallas_call x1, Pallas kernels: 5.58 us -> 3.74 us  [levels(): pl.pallas_call(levels_kernel, out_shape=[jax.ShapeDtypeStruct((leaves, wi...]
  transfers between devices with their start and end apart: 3 -> 3, of which waited for: 1 -> 1; matrix products, arithmetic and copies ran while one was open for 0% -> 0% of each run, Pallas kernels for 49% -> 38%
where the time goes in v2:
time: 76.6 us; the launch traced here: 76.3 us
  Pallas kernels  39.3 us (51%)
  starting transfers between devices  23.3 us (30%)
  waiting for transfers between devices  12.8 us (17%)
  between operations  0.9 us (1%)
    ppermute x1, waiting for transfers between devices, shards(): other = lax.ppermute(own, 'grp', [(i, i ^ 1) for i in range(size)])  12.8 us
    all_to_all x1, starting transfers between devices, shards(): asked = lax.all_to_all(tags, BOTH, split_axis=0, concat_axis=0, tiled=True)  11.5 us
    all_to_all x1, starting transfers between devices, shards(): lax.all_to_all(answers, BOTH, split_axis=0, concat_axis=0, tiled=True)  10.2 us
    pallas_call x1, Pallas kernels, leaf_factors(): pl.pallas_call(functools.partial(factor_kernel, leaves, width), in_specs=...  9.73 us
    pallas_call x1, Pallas kernels, finish(): pl.pallas_call(finish_kernel, in_specs=[scalar, scalar, HBM, VMEM], out_s...  6.76 us
    pallas_call x1, Pallas kernels, level_one(): pl.pallas_call(one_kernel, in_specs=[VMEM] * 3, out_specs=[VMEM] * 2, out...  4.62 us
    pallas_call x1, Pallas kernels, level_two(): pl.pallas_call(two_kernel, in_specs=[VMEM] * 3, out_specs=VMEM, out_shape...  4.23 us
    pallas_call x1, Pallas kernels, levels(): pl.pallas_call(levels_kernel, out_shape=[jax.ShapeDtypeStruct((leaves, wi...  3.74 us
  transfers between devices with their start and end apart: 3, of which 1 were waited for; matrix products, arithmetic and copies ran while one was open for 0% of the time, Pallas kernels for 38%

profile of v2, /device:TPU:1, one launch (start us, length us, event | category | flops | bytes accessed | tf_op | source)
XLA Modules:
  0.0 76.3 jit_solution(15923989380938848511)
XLA Ops:
  0.6 1.6 %requests.1 = (s32[128,128]{1,0:T(8,128)}, s32[1,128]{1,0:T(1,128)}) custom-call(s32[1,128]{1,0:T(1,128)} %bitcast.45, s32[1,128]{1,0:T(1,128)} %bitcast.48), custom_call_target="tpu_custom_call" | custom-call | flops 100000 | bytes 100000 | tf_op jit(solution)/shard_map/requests/pallas_call | solution.py:137
  2.2 11.5 %all-to-all-start = ((s32[128,1,128]{2,1,0:T(1,128)}), s32[128,1,128]{2,1,0:T(1,128)S(1)}, u32[]{:S(2)}, u32[]{:S(2)}) async-start(s32[128,1,128]{2,1,0:T(1,128)} %bitcast.47), calls=%async_computation | async-start | bytes 131072 | tf_op jit(solution)/shard_map/all_to_all | solution.py:595
  13.7 9.7 %leaf_factors.1 = (f32[16,64,128]{2,1,0:T(8,128)S(1)}, bf16[16,64,192]{2,1,0:T(8,128)(2,1)S(1)}, f32[16,40,128]{2,1,0:T(8,128)S(1)}, f32[16,40,128]{2,1,0:T(8,128)S(1)}) custom-call(f32[16,64,1024]{2,1,0:T(8,128)} %basis_ref.1), custom_call_target="tpu_custom_call" | custom-call | flops 5000000000 | bytes 6000000 | tf_op jit(solution)/shard_map/leaf_factors/pallas_call | solution.py:217
  23.4 0.0 all-to-all-done
  23.4 2.3 %replies.1 = f32[4608,128]{1,0:T(8,128)} custom-call(s32[128,128]{1,0:T(8,128)S(1)} %bitcast.39, f32[16,40,128]{2,1,0:T(8,128)S(1)} %get-tuple-element.24.pack_ref, f32[16,40,128]{2,1,0:T(8,128)S(1)} %get-tuple-element.25.pack_up_ref), custom_call_target="tpu_custom_call" | custom-call | flops 1000000 | bytes 4000000 | tf_op jit(solution)/shard_map/replies/pallas_call | solution.py:264
  25.8 0.0 copy-start.2
  25.8 0.0 copy-start.3
  25.8 10.2 %all-to-all-start.1 = ((f32[128,1,4608]{2,1,0:T(1,128)}), f32[128,1,4608]{2,1,0:T(1,128)}, u32[]{:S(2)}, u32[]{:S(2)}) async-start(f32[128,1,4608]{2,1,0:T(1,128)} %bitcast.21), calls=%async_computation.1 | async-start | bytes 4718592 | tf_op jit(solution)/shard_map/all_to_all | solution.py:598
  36.0 0.0 copy-done.2
  36.0 0.0 copy-done.3
  36.0 0.0 copy-start
  36.0 3.7 %levels.1 = (f32[16,64,64]{2,1,0:T(8,128)S(1)}, f32[8,64,64]{2,1,0:T(8,128)S(1)}, f32[4,64,128]{2,1,0:T(8,128)S(1)}) custom-call(bf16[16,64,192]{2,1,0:T(8,128)(2,1)S(1)} %get-tuple-element.16.triple_ref, f32[512,128]{1,0:T(8,128)S(1)} %bitcast.41, f32[256,128]{1,0:T(8,128)S(1)} %bitcast.42), custom_call_target="tpu_custom_call" | custom-call | flops 5000000000 | bytes 2000000 | tf_op jit(solution)/shard_map/levels/pallas_call | solution.py:327
  39.8 1.6 %collective-permute-start = (f32[4,64,128]{2,1,0:T(8,128)S(1)}, f32[4,64,128]{2,1,0:T(8,128)S(1)}, u32[]{:S(2)}, u32[]{:S(2)}) collective-permute-start(f32[4,64,128]{2,1,0:T(8,128)S(1)} %get-tuple-element.20.own_ref), channel_id=1, source_target_pairs={{0,32},{32,0},{64,96},{96,64},{1,33},{33,1},{65,97},{97,65},{2,34}... | collective-permute-start | bytes 393224 | tf_op jit(solution)/shard_map/ppermute | solution.py:603
  41.4 0.0 copy-done
  41.4 2.9 %ortho.1 = f32[16,64,1024]{2,1,0:T(8,128)} custom-call(f32[16,64,128]{2,1,0:T(8,128)S(1)} %get-tuple-element.15.rl_ref, f32[16,64,1024]{2,1,0:T(8,128)S(1)} %copy-done), custom_call_target="tpu_custom_call" | custom-call | flops 5000000000 | bytes 8000000 | tf_op jit(solution)/shard_map/ortho/pallas_call | solution.py:416
  44.2 0.0 copy-done.1
  44.2 0.0 copy-done.4
  44.2 3.5 %lefts.1.left_hbm = bf16[64,128,128]{2,1,0:T(8,128)(2,1)S(1)} custom-call(s32[1,128]{1,0:T(1,128)S(1)} %bitcast.44, bf16[16,64,192]{2,1,0:T(8,128)(2,1)S(1)} %get-tuple-element.16.triple_ref, f32[4096,128]{1,0:T(8,128)S(1)} %bitcast.40), custom_call_target="tpu_custom_call" | custom-call | flops 5000000000 | bytes 6000000 | tf_op jit(solution)/shard_map/lefts/pallas_call | solution.py:460
  47.7 0.0 copy-start.7
  47.7 4.6 %level_one.1 = (f32[512,128]{1,0:T(8,128)}, f32[8,64,64]{2,1,0:T(8,128)S(1)}) custom-call(f32[8,64,64]{2,1,0:T(8,128)S(1)} %get-tuple-element.17.one_ref, f32[16,64,64]{2,1,0:T(8,128)S(1)} %get-tuple-element.18.lifted_ref, f32[256,128]{1,0:T(8,128)S(1)} %bitcast.43), custom_call_target="tpu_custom_call" | custom-call | flops 3000000000 | bytes 2000000 | tf_op jit(solution)/shard_map/level_one/pallas_call | solution.py:362
  52.4 12.8 %collective-permute-done.other_ref = f32[4,64,128]{2,1,0:T(8,128)S(1)} collective-permute-done((f32[4,64,128]{2,1,0:T(8,128)S(1)}, f32[4,64,128]{2,1,0:T(8,128)S(1)}, u32[]{:S(2)}, u32[]{:S(2)}) %collective-permute-start) | collective-permute-done | bytes 131104 | tf_op jit(solution)/shard_map/ppermute | solution.py:603
  65.1 4.2 %level_two.1 = f32[256,128]{1,0:T(8,128)} custom-call(f32[4,64,128]{2,1,0:T(8,128)S(1)} %get-tuple-element.20.own_ref, f32[4,64,128]{2,1,0:T(8,128)S(1)} %collective-permute-done.other_ref, f32[8,64,64]{2,1,0:T(8,128)S(1)} %get-tuple-element.21.raised_ref), custom_call_target="tpu_custom_call" | custom-call | flops 1000000000 | bytes 1000000 | tf_op jit(solution)/shard_map/level_two/pallas_call | solution.py:396
  69.4 0.0 all-to-all-done.1
  69.4 6.8 %finish.1 = f32[4096,128]{1,0:T(8,128)} custom-call(s32[1,128]{1,0:T(1,128)S(1)} %bitcast.46, s32[1,128]{1,0:T(1,128)S(1)} %copy-done.6, bf16[64,128,128]{2,1,0:T(8,128)(2,1)} %copy-done.7, f32[4608,128]{1,0:T(8,128)} %bitcast.22.pack_ref), custom_call_target="tpu_custom_call" | custom-call | flops 5000000000 | bytes 8000000 | tf_op jit(solution)/shard_map/finish/pallas_call | solution.py:562
  (7 shorter events, 0.0 us)
Async XLA Ops:
  2.2 21.2 %all-to-all-start = ((s32[128,1,128]{2,1,0:T(1,128)}), s32[128,1,128]{2,1,0:T(1,128)S(1)}, u32[]{:S(2)}, u32[]{:S(2)}) async-start(s32[128,1,128]{2,1,0:T(1,128)} %bitcast.47), calls=%async_computation | async-start | bytes 131072 | tf_op jit(solution)/shard_map/all_to_all | solution.py:595
  25.8 10.2 %copy-start.2 = (f32[16,4096]{1,0:T(8,128)S(1)}, f32[16,4096]{1,0:T(8,128)}, u32[]{:S(2)}) copy-start(f32[16,4096]{1,0:T(8,128)} %param.8) | copy-start | bytes 786436
  25.8 10.2 %copy-start.3 = (f32[8,4096]{1,0:T(8,128)S(1)}, f32[8,4096]{1,0:T(8,128)}, u32[]{:S(2)}) copy-start(f32[8,4096]{1,0:T(8,128)} %param.9) | copy-start | bytes 393220
  25.8 43.6 %all-to-all-start.1 = ((f32[128,1,4608]{2,1,0:T(1,128)}), f32[128,1,4608]{2,1,0:T(1,128)}, u32[]{:S(2)}, u32[]{:S(2)}) async-start(f32[128,1,4608]{2,1,0:T(1,128)} %bitcast.21), calls=%async_computation.1 | async-start | bytes 4718592 | tf_op jit(solution)/shard_map/all_to_all | solution.py:598
  36.0 5.4 %copy-start = (f32[16,64,1024]{2,1,0:T(8,128)S(1)}, f32[16,64,1024]{2,1,0:T(8,128)}, u32[]{:S(2)}) copy-start(f32[16,64,1024]{2,1,0:T(8,128)} %basis_ref.1) | copy-start | bytes 12582916
  39.8 25.4 %collective-permute-start = (f32[4,64,128]{2,1,0:T(8,128)S(1)}, f32[4,64,128]{2,1,0:T(8,128)S(1)}, u32[]{:S(2)}, u32[]{:S(2)}) collective-permute-start(f32[4,64,128]{2,1,0:T(8,128)S(1)} %get-tuple-element.20.own_ref), channel_id=1, source_target_pairs={{0,32},{32,0},{64,96},{96,64},{1,33},{33,1},{65,97},{97,65},{2,34}... | collective-permute-start | bytes 393224 | tf_op jit(solution)/shard_map/ppermute | solution.py:603
  41.4 2.9 %copy-start.1 = (f32[128,4096]{1,0:T(8,128)S(1)}, f32[128,4096]{1,0:T(8,128)}, u32[]{:S(2)}) copy-start(f32[128,4096]{1,0:T(8,128)} %param.10) | copy-start | bytes 6291460
  41.4 2.9 %copy-start.4 = (s32[128]{0:T(128)S(1)}, s32[128]{0:T(128)}, u32[]{:S(2)}) copy-start(s32[128]{0:T(128)} %param.11) | copy-start | bytes 1540
  47.7 4.6 %copy-start.7 = (bf16[64,128,128]{2,1,0:T(8,128)(2,1)}, bf16[64,128,128]{2,1,0:T(8,128)(2,1)S(1)}, u32[]{:S(2)}) copy-start(bf16[64,128,128]{2,1,0:T(8,128)(2,1)S(1)} %lefts.1.left_hbm) | copy-start | bytes 6291460
  52.4 17.0 %copy-start.5 = (s32[128,1]{0,1:T(1,128)S(1)}, s32[128,1]{0,1:T(1,128)}, u32[]{:S(2)}) copy-start(s32[128,1]{0,1:T(1,128)} %param.12) | copy-start | bytes 1540
  52.4 17.0 %copy-start.6 = (s32[1,128]{1,0:T(1,128)S(1)}, s32[1,128]{1,0:T(1,128)}, u32[]{:S(2)}) copy-start(s32[1,128]{1,0:T(1,128)} %get-tuple-element.22.place_ref) | copy-start | bytes 1540

commit v3 on v2

--- a/solution.py
+++ b/solution.py
@@ -9,7 +9,7 @@
 from jax.sharding import PartitionSpec as P
 
 BOTH = ("grp", "dev")
-ROWS = 36
+ROWS = 34
 ROOM = pltpu.CompilerParams(vmem_limit_bytes=24 << 20)
 VMEM = pl.BlockSpec(memory_space=pltpu.VMEM)
 HBM = pl.BlockSpec(memory_space=pltpu.HBM)
@@ -146,23 +146,24 @@
 
 
 def pack_rows(lower):
-    moved = lambda start, stop, lane: pltpu.roll(lower[start:stop], lane, 1)
-    quarter = lower[24:32]
-    last = quarter + pltpu.roll(pltpu.roll(quarter, 4, 0), 32, 1)
+    v = [lower[8 * k : 8 * k + 8] for k in range(8)]
+    row = sublanes(v[0].shape)
+    moved = lambda x, lane: pltpu.roll(x, lane, 1)
+    ends = pltpu.roll(v[3], 4, 0) + moved(pltpu.roll(v[3], 2, 0), 32)
     return jnp.concatenate(
         [
-            lower[56:64],
-            lower[48:56] + moved(0, 8, 56),
-            lower[40:48] + moved(8, 16, 48),
-            lower[32:40] + moved(16, 24, 40),
-            jnp.where(sublanes(last.shape) < 4, last, 0.0),
+            v[7] + jnp.where(row < 4, moved(v[0], 60), 0.0),
+            v[6] + jnp.where(row < 4, moved(v[1], 52), moved(v[0], 56)),
+            v[5] + jnp.where(row < 4, moved(v[2], 44), moved(v[1], 48)),
+            v[4] + jnp.where(row < 4, moved(v[3], 36), moved(v[2], 40)),
+            jnp.where(row < 2, ends, 0.0),
         ],
         axis=0,
     )
 
 
 def factor_kernel(
-    leaves, width, source_ref, rl_ref, triple_ref, pack_ref, pack_up_ref, work, basis_ref, sems
+    leaves, width, source_ref, rows_ref, pack_ref, pack_up_ref, work, basis_ref, sems
 ):
     count, _, points = basis_ref.shape
     pieces = sems.shape[0]
@@ -187,27 +188,13 @@
         work[pl.ds(q + 1, width, stride=leaves), :] = with_identity(
             pltpu.roll(gram[width:], width, 1)
         )
-
     eliminate(work, width, leaves)
+    rows_ref[...] = work[...]
     lane = lanes((two, two))
-    half = width // 2
-    target = lanes((two, width))
-    source = jnp.where(target < half, 2 * target, 2 * (target - half) + 1)
-    reorder = (sublanes((two, width)) == source).astype(f32).astype(bf16)
     for b in range(leaves):
         whole = work[pl.ds(b, width, stride=leaves), :]
-        rl_ref[b] = whole
-        even = work[pl.ds(b, half, stride=2 * leaves), :]
-        odd = work[pl.ds(b + leaves, half, stride=2 * leaves), :]
-        high, low = halves(jnp.concatenate([even, odd], axis=0))
-        both = jnp.concatenate([high, low], axis=0).astype(bf16)
-        moved = jnp.dot(both, reorder, preferred_element_type=f32)
-        triple_ref[b] = jnp.concatenate(
-            [moved[:width], moved[:width], moved[width:]], axis=1
-        ).astype(bf16)
         padded = jnp.concatenate([whole, jnp.zeros_like(whole)], axis=0)
-        lower = jnp.where(lane < width, padded, 0.0).T[:width]
-        pack = pack_rows(lower)
+        pack = pack_rows(jnp.where(lane < width, padded, 0.0).T[:width])
         pack_ref[b] = pack
         pack_up_ref[b] = pltpu.roll(pack, width, 1)
 
@@ -217,19 +204,18 @@
     return pl.pallas_call(
         functools.partial(factor_kernel, leaves, width),
         in_specs=[HBM],
-        out_specs=[VMEM] * 4,
+        out_specs=[VMEM] * 3,
         out_shape=[
-            jax.ShapeDtypeStruct((leaves, width, 2 * width), f32),
-            jax.ShapeDtypeStruct((leaves, width, 3 * width), bf16),
+            jax.ShapeDtypeStruct((width * leaves, 2 * width), f32),
             jax.ShapeDtypeStruct((leaves, 40, 2 * width), f32),
             jax.ShapeDtypeStruct((leaves, 40, 2 * width), f32),
         ],
         scratch_shapes=[
             pltpu.VMEM((width * leaves, 2 * width), f32),
             pltpu.VMEM(basis.shape, f32),
-            pltpu.SemaphoreType.DMA((leaves // 4,)),
-        ],
-        compiler_params=pltpu.CompilerParams(vmem_limit_bytes=53248 << 10),
+            pltpu.SemaphoreType.DMA((leaves // 8,)),
+        ],
+        compiler_params=pltpu.CompilerParams(vmem_limit_bytes=52 << 20),
         cost_estimate=cost(5e9, 6e6),
         name="leaf_factors",
     )(basis)
@@ -246,14 +232,19 @@
         copy.start()
         copy.wait()
 
-    for r in range(0, count, 2):
-        at = step * count + r
-        even = pack_ref[table[0, at]] + pack_up_ref[table[1, at]]
-        odd = pack_ref[table[0, at + 1]] + pack_up_ref[table[1, at + 1]]
-        odd = pltpu.roll(odd, 4, 0)
-        out_ref[r * ROWS : r * ROWS + 32] = even[:32]
-        out_ref[r * ROWS + 32 : r * ROWS + 40] = even[32:] + odd[:8]
-        out_ref[r * ROWS + 40 : (r + 2) * ROWS] = odd[8:]
+    for r in range(0, count, 4):
+        parts = []
+        for k in range(4):
+            at = step * count + r + k
+            part = pack_ref[table[0, at]] + pack_up_ref[table[1, at]]
+            parts.append(pltpu.roll(part, 2 * k, 0) if k else part)
+        base = r * ROWS
+        out_ref[base : base + 32] = parts[0][:32]
+        for k in range(1, 4):
+            edge = base + 32 * k
+            out_ref[edge : edge + 8] = parts[k - 1][32:] + parts[k][:8]
+            out_ref[edge + 8 : edge + 32] = parts[k][8:32]
+        out_ref[base + 128 : base + 136] = parts[3][32:]
 
 
 def replies(tags, pack, pack_up):
@@ -299,15 +290,30 @@
     return scratch[:, : wide // 2]
 
 
-def levels_kernel(triple_ref, leaf_ref, upper_ref, lifted_ref, one_ref, two_ref, scratch):
-    leaves = triple_ref.shape[0]
+def levels_kernel(
+    work, leaf_ref, upper_ref, triple_ref, lifted_ref, one_ref, two_ref, scratch
+):
+    leaves, width, _ = triple_ref.shape
+    two, half = 2 * width, width // 2
+    target = lanes((two, width))
+    source = jnp.where(target < half, 2 * target, 2 * (target - half) + 1)
+    reorder = (sublanes((two, width)) == source).astype(f32).astype(bf16)
     kept = None
     for c in range(leaves // 2):
         upper = natural(pair_of(upper_ref, c), scratch.at[c])
         lifted = []
         for n in (2 * c, 2 * c + 1):
+            even = work[pl.ds(n, half, stride=2 * leaves), :]
+            odd = work[pl.ds(n + leaves, half, stride=2 * leaves), :]
+            high, low = halves(jnp.concatenate([even, odd], axis=0))
+            both = jnp.concatenate([high, low], axis=0).astype(bf16)
+            moved = jnp.dot(both, reorder, preferred_element_type=f32)
+            triple = jnp.concatenate(
+                [moved[:width], moved[:width], moved[width:]], axis=1
+            ).astype(bf16)
+            triple_ref[n] = triple
             here = jnp.dot(
-                triple_ref[n],
+                triple,
                 right_triple(split_rows(pair_of(leaf_ref, n))),
                 preferred_element_type=f32,
             )
@@ -322,20 +328,25 @@
         kept = second
 
 
-def levels(triple, leaf_pairs, upper_pairs):
-    leaves, width, _ = triple.shape
+def levels(work, leaf_pairs, upper_pairs):
+    rows, wide = work.shape
+    width = wide // 2
+    leaves = rows // width
     return pl.pallas_call(
         levels_kernel,
+        in_specs=[VMEM] * 3,
+        out_specs=[VMEM] * 4,
         out_shape=[
+            jax.ShapeDtypeStruct((leaves, width, 3 * width), bf16),
             jax.ShapeDtypeStruct((leaves, width, width), f32),
             jax.ShapeDtypeStruct((leaves // 2, width, width), f32),
-            jax.ShapeDtypeStruct((leaves // 4, width, 2 * width), f32),
-        ],
-        scratch_shapes=[pltpu.VMEM((leaves // 2, width, 2 * width), f32)],
+            jax.ShapeDtypeStruct((leaves // 4, width, wide), f32),
+        ],
+        scratch_shapes=[pltpu.VMEM((leaves // 2, width, wide), f32)],
         compiler_params=ROOM,
         cost_estimate=cost(5e9, 2e6),
         name="levels",
-    )(triple, leaf_pairs, upper_pairs)
+    )(work, leaf_pairs, upper_pairs)
 
 
 def one_kernel(one_ref, lifted_ref, upper_ref, leaf_out, raised_out, work, scratch):
@@ -405,68 +416,69 @@
     )(own, other, raised)
 
 
-def ortho_kernel(factor, rl_ref, basis_ref, out_ref):
-    width = basis_ref.shape[1]
-    for n in range(basis_ref.shape[0]):
-        out_ref[n] = product(rl_ref[n][:, width:] * factor, basis_ref[n])
-
-
-def ortho(rl, basis):
+def ortho_kernel(factor, work, basis_ref, out_ref):
+    count, width, _ = basis_ref.shape
+    leaves = work.shape[0] // width
+    step = pl.program_id(0)
+    for n in range(count):
+        inverse = work[pl.ds(step * count + n, width, stride=leaves), :][:, width:]
+        out_ref[n] = product(inverse * factor, basis_ref[n])
+
+
+def ortho(work, basis):
     leaves, width, points = basis.shape
+    part = pl.BlockSpec((leaves // 2, width, points), lambda i: (i, 0, 0))
     return pl.pallas_call(
         functools.partial(ortho_kernel, math.sqrt(points)),
         grid=(2,),
-        in_specs=[
-            pl.BlockSpec((leaves // 2, width, 2 * width), lambda i: (i, 0, 0)),
-            pl.BlockSpec((leaves // 2, width, points), lambda i: (i, 0, 0)),
-        ],
-        out_specs=pl.BlockSpec((leaves // 2, width, points), lambda i: (i, 0, 0)),
+        in_specs=[VMEM, part],
+        out_specs=part,
         out_shape=jax.ShapeDtypeStruct(basis.shape, f32),
         compiler_params=ROOM,
         cost_estimate=cost(5e9, 8e6),
         name="ortho",
-    )(rl, basis)
-
-
-def left_kernel(row_ref, triple_ref, coupling_ref, out_ref):
-    step = pl.program_id(0)
-    count = 2 * out_ref.shape[0]
-
-    def group(g, _):
-        for q in range(16):
-            at = g * 32 + 2 * q
+    )(work, basis)
+
+
+def left_kernel(row_ref, triple_ref, coupling_ref, first_ref, later_ref):
+    size = first_ref.shape[0]
+
+    def group(g, out_ref, start):
+        for q in range(size):
             pair = []
             for i in range(2):
-                block = coupling_ref[pl.ds(g * 1024 + q // 4 * 256 + (2 * q + i) % 8, 32, stride=8), :]
+                at = (g * size + q) * 2 + i
+                base = g * size * 64 + q // 4 * 256 + (2 * q + i) % 8
                 pair.append(
                     jnp.dot(
-                        triple_ref[row_ref[0, step * count + at + i]],
-                        right_triple(split_rows(block)),
+                        triple_ref[row_ref[0, at]],
+                        right_triple(split_rows(coupling_ref[pl.ds(base, 32, stride=8), :])),
                         preferred_element_type=f32,
                     )
                 )
             high, low = halves(jnp.concatenate(pair, axis=1))
-            out_ref[g * 16 + q] = jnp.concatenate([high, low], axis=0).astype(bf16)
+            out_ref[start + q] = jnp.concatenate([high, low], axis=0).astype(bf16)
+
+    group(0, first_ref, 0)
+
+    def later(g, _):
+        group(g, later_ref, (g - 1) * size)
         return 0
 
-    lax.fori_loop(0, count // 32, group, 0)
+    lax.fori_loop(1, 1 + later_ref.shape[0] // size, later, 0)
 
 
 def lefts(row_leaf, triple, coupling_pairs):
     blocks = row_leaf.shape[1]
-    leaves, width, _ = triple.shape
-    wide = 2 * width
-    per = blocks // 2
+    wide = 2 * triple.shape[1]
     return pl.pallas_call(
         left_kernel,
-        grid=(blocks // per,),
-        in_specs=[
-            pl.BlockSpec(memory_space=pltpu.SMEM),
-            pl.BlockSpec(triple.shape, lambda i: (0, 0, 0)),
-            pl.BlockSpec((per * width // 2, wide), lambda i: (i, 0)),
-        ],
-        out_specs=pl.BlockSpec((per // 2, wide, wide), lambda i: (i, 0, 0)),
-        out_shape=jax.ShapeDtypeStruct((blocks // 2, wide, wide), bf16),
+        in_specs=[pl.BlockSpec(memory_space=pltpu.SMEM), VMEM, VMEM],
+        out_specs=[VMEM] * 2,
+        out_shape=[
+            jax.ShapeDtypeStruct((blocks // 8, wide, wide), bf16),
+            jax.ShapeDtypeStruct((3 * blocks // 8, wide, wide), bf16),
+        ],
         compiler_params=ROOM,
         cost_estimate=cost(5e9, 6e6),
         name="lefts",
@@ -474,65 +486,60 @@
 
 
 def unpack(ref, base, place, side):
-    lane = lanes((8, 128)) - 64 * side
+    lane, row = lanes((8, 128)) - 64 * side, sublanes((8, 128))
     shift = (place ^ side) * 64
-
-    def piece(rows, start, count):
-        turned = pltpu.roll(rows, lax.rem(shift + (128 - start), 128), 1)
-        return jnp.where((lane >= 0) & (lane < count), turned, 0.0)
-
-    first, second, third, fourth = [ref[pl.ds(base + 8 * k, 8), :] for k in range(4)]
-    last = ref[pl.ds(base + 28, 8), :]
-    middle = jnp.where(
-        sublanes((8, 128)) < 4,
-        pltpu.roll(piece(last, 0, 32), 4, 0),
-        piece(last, 32, 32),
-    )
+    turn = lambda x, start: pltpu.roll(x, lax.rem(shift + (128 - start), 128), 1)
+    p = [ref[pl.ds(base + 8 * k, 8), :] for k in range(4)]
+    last = ref[pl.ds(base + 26, 8), :]
+    middle = jnp.where(row < 6, pltpu.roll(turn(last, 0), 6, 0), turn(last, 32))
+    found = [
+        jnp.where(row < 4, turn(p[0], 60), turn(p[1], 56)),
+        jnp.where(row < 4, turn(p[1], 52), turn(p[2], 48)),
+        jnp.where(row < 4, turn(p[2], 44), turn(p[3], 40)),
+        jnp.where(row < 4, turn(p[3], 36), middle),
+        turn(p[3], 0),
+        turn(p[2], 0),
+        turn(p[1], 0),
+        turn(p[0], 0),
+    ]
+    reach = jnp.where(row < 4, 4, 8)
     return jnp.concatenate(
         [
-            piece(second, 56, 8),
-            piece(third, 48, 16),
-            piece(fourth, 40, 24),
-            middle,
-            piece(fourth, 0, 40),
-            piece(third, 0, 48),
-            piece(second, 0, 56),
-            piece(first, 0, 64),
+            jnp.where((lane >= 0) & (lane < reach + 8 * k), x, 0.0)
+            for k, x in enumerate(found)
         ],
         axis=0,
     )
 
 
 def finish_kernel(
-    dest_ref, place_ref, left_hbm, pack_ref, out_hbm, left_ref, out_ref, in_sems, out_sems
+    dest_ref, place_ref, first_ref, later_hbm, pack_ref, out_hbm, later_ref, out_ref, in_sems, out_sems
 ):
-    pairs, wide, _ = left_ref.shape
+    size, wide, _ = first_ref.shape
     width = wide // 2
     lane = lanes((width // 2, wide))
-    groups = in_sems.shape[0]
-    size = pairs // groups
+    groups = out_sems.shape[0]
     rows = size * wide // 2
 
     def fetch(g):
-        part = pl.ds(g * size, size)
-        return pltpu.make_async_copy(left_hbm.at[part], left_ref.at[part], in_sems.at[g])
+        part = pl.ds((g - 1) * size, size)
+        return pltpu.make_async_copy(later_hbm.at[part], later_ref.at[part], in_sems.at[g - 1])
 
     def put(g):
         part = pl.ds(pl.multiple_of(g * rows, rows), rows)
         return pltpu.make_async_copy(out_ref.at[part], out_hbm.at[part], out_sems.at[g])
 
-    for g in range(groups):
+    for g in range(1, groups):
         fetch(g).start()
 
-    def group(g, _):
-        fetch(g).wait()
+    def group(g, left_ref, start):
         for q in range(size):
             lower = []
             for i in range(2):
                 at = (g * size + q) * 2 + i
                 lower.append(unpack(pack_ref, dest_ref[0, at] * ROWS, place_ref[0, at], i))
             high, low = halves(jnp.concatenate(lower, axis=0))
-            left = left_ref[g * size + q]
+            left = left_ref[start + q]
             both = jnp.dot(left, high.astype(bf16), preferred_element_type=f32)
             done = (
                 both[:width]
@@ -548,32 +555,40 @@
                 lane < width, pltpu.roll(even, width, 1), odd
             )
         put(g).start()
+
+    group(0, first_ref, 0)
+
+    def later(g, _):
+        fetch(g).wait()
+        group(g, later_ref, (g - 1) * size)
         return 0
 
-    lax.fori_loop(0, groups, group, 0)
+    lax.fori_loop(1, groups, later, 0)
     for g in range(groups):
         put(g).wait()
 
 
 def finish(dests, place, left, packs):
-    pairs, wide, _ = left.shape
+    first, later = left
+    size, wide, _ = first.shape
+    pairs = size + later.shape[0]
     scalar = pl.BlockSpec(memory_space=pltpu.SMEM)
     shape = (pairs * wide // 2, wide)
     return pl.pallas_call(
         finish_kernel,
-        in_specs=[scalar, scalar, HBM, VMEM],
+        in_specs=[scalar, scalar, VMEM, HBM, VMEM],
         out_specs=HBM,
         out_shape=jax.ShapeDtypeStruct(shape, f32),
         scratch_shapes=[
-            pltpu.VMEM(left.shape, bf16),
+            pltpu.VMEM(later.shape, bf16),
             pltpu.VMEM(shape, f32),
-            pltpu.SemaphoreType.DMA((4,)),
-            pltpu.SemaphoreType.DMA((4,)),
-        ],
-        compiler_params=pltpu.CompilerParams(vmem_limit_bytes=53248 << 10),
+            pltpu.SemaphoreType.DMA((pairs // size - 1,)),
+            pltpu.SemaphoreType.DMA((pairs // size,)),
+        ],
+        compiler_params=pltpu.CompilerParams(vmem_limit_bytes=50 << 20),
         cost_estimate=cost(5e9, 8e6),
         name="finish",
-    )(dests, place, left, packs)
+    )(dests, place, first, later, packs)
 
 
 def to_pairs(rows):
@@ -593,16 +608,16 @@
     dests = col_dev.reshape(1, blocks)
     tags, place = requests(dests, col_leaf.reshape(1, blocks))
     asked = lax.all_to_all(tags, BOTH, split_axis=0, concat_axis=0, tiled=True)
-    rl, triple, pack, pack_up = leaf_factors(basis)
+    work, pack, pack_up = leaf_factors(basis)
     answers = replies(asked, pack, pack_up).reshape(asked.shape[0], 1, -1)
     packs = lax.all_to_all(answers, BOTH, split_axis=0, concat_axis=0, tiled=True)
     packs = packs.reshape(-1, pack.shape[2])
     upper_pairs = to_pairs(upper_transfer)
-    lifted, one, own = levels(triple, to_pairs(leaf_transfer), upper_pairs)
+    triple, lifted, one, own = levels(work, to_pairs(leaf_transfer), upper_pairs)
     size = lax.axis_size("grp")
     other = lax.ppermute(own, "grp", [(i, i ^ 1) for i in range(size)])
     left = lefts(row_leaf.reshape(1, blocks), triple, to_pairs(coupling))
-    ortho_basis = ortho(rl, basis)
+    ortho_basis = ortho(work, basis)
     leaf_out, raised = level_one(one, lifted, upper_pairs)
     upper_out = level_two(own, other, raised)
     coupling_out = finish(dests, place, left, packs)

time: 76.6 us -> 75.2 us (0.982)
  waiting for transfers between devices: 12.8 us -> 11.1 us
    ppermute x1, waiting for transfers between devices: 12.8 us -> 11.1 us  [shards(): other = lax.ppermute(own, 'grp', [(i, i ^ 1) for i in range(size)])]
where the time goes in v3:
time: 75.2 us; the launch traced here: 75 us
  Pallas kernels  39.7 us (53%)
  starting transfers between devices  23.3 us (31%)
  waiting for transfers between devices  11.1 us (15%)
  between operations  0.91 us (1%)
    all_to_all x1, starting transfers between devices, shards(): asked = lax.all_to_all(tags, BOTH, split_axis=0, concat_axis=0, tiled=True)  11.5 us
    ppermute x1, waiting for transfers between devices, shards(): other = lax.ppermute(own, 'grp', [(i, i ^ 1) for i in range(size)])  11.1 us
    all_to_all x1, starting transfers between devices, shards(): lax.all_to_all(answers, BOTH, split_axis=0, concat_axis=0, tiled=True)  10.2 us
    pallas_call x1, Pallas kernels, leaf_factors(): pl.pallas_call(functools.partial(factor_kernel, leaves, width), in_specs=...  9.66 us
    pallas_call x1, Pallas kernels, finish(): pl.pallas_call(finish_kernel, in_specs=[scalar, scalar, VMEM, HBM, VMEM],...  7 us
    pallas_call x1, Pallas kernels, level_one(): pl.pallas_call(one_kernel, in_specs=[VMEM] * 3, out_specs=[VMEM] * 2, out...  4.62 us
    pallas_call x1, Pallas kernels, level_two(): pl.pallas_call(two_kernel, in_specs=[VMEM] * 3, out_specs=VMEM, out_shape...  4.23 us
    pallas_call x1, Pallas kernels, levels(): pl.pallas_call(levels_kernel, in_specs=[VMEM] * 3, out_specs=[VMEM] * 4,...  3.94 us
  transfers between devices with their start and end apart: 3, of which 1 were waited for; matrix products, arithmetic and copies ran while one was open for 0% of the time, Pallas kernels for 38%

profile of v3, /device:TPU:1, one launch (start us, length us, event | category | flops | bytes accessed | tf_op | source)
XLA Modules:
  0.0 75.0 jit_solution(15567615264876847472)
XLA Ops:
  0.6 1.6 %requests.1 = (s32[128,128]{1,0:T(8,128)}, s32[1,128]{1,0:T(1,128)}) custom-call(s32[1,128]{1,0:T(1,128)} %bitcast.45, s32[1,128]{1,0:T(1,128)} %bitcast.48), custom_call_target="tpu_custom_call" | custom-call | flops 100000 | bytes 100000 | tf_op jit(solution)/shard_map/requests/pallas_call | solution.py:137
  2.2 11.5 %all-to-all-start = ((s32[128,1,128]{2,1,0:T(1,128)}), s32[128,1,128]{2,1,0:T(1,128)S(1)}, u32[]{:S(2)}, u32[]{:S(2)}) async-start(s32[128,1,128]{2,1,0:T(1,128)} %bitcast.47), calls=%async_computation | async-start | bytes 131072 | tf_op jit(solution)/shard_map/all_to_all | solution.py:610
  13.7 9.7 %leaf_factors.1 = (f32[1024,128]{1,0:T(8,128)S(1)}, f32[16,40,128]{2,1,0:T(8,128)S(1)}, f32[16,40,128]{2,1,0:T(8,128)S(1)}) custom-call(f32[16,64,1024]{2,1,0:T(8,128)} %basis_ref.1), custom_call_target="tpu_custom_call" | custom-call | flops 5000000000 | bytes 6000000 | tf_op jit(solution)/shard_map/leaf_factors/pallas_call | solution.py:204
  23.3 0.0 all-to-all-done
  23.4 2.3 %replies.1 = f32[4352,128]{1,0:T(8,128)} custom-call(s32[128,128]{1,0:T(8,128)S(1)} %bitcast.39, f32[16,40,128]{2,1,0:T(8,128)S(1)} %get-tuple-element.28.pack_ref, f32[16,40,128]{2,1,0:T(8,128)S(1)} %get-tuple-element.29.pack_up_ref), custom_call_target="tpu_custom_call" | custom-call | flops 1000000 | bytes 4000000 | tf_op jit(solution)/shard_map/replies/pallas_call | solution.py:255
  25.7 0.0 copy-start.2
  25.7 0.0 copy-start.3
  25.7 10.2 %all-to-all-start.1 = ((f32[128,1,4352]{2,1,0:T(1,128)}), f32[128,1,4352]{2,1,0:T(1,128)}, u32[]{:S(2)}, u32[]{:S(2)}) async-start(f32[128,1,4352]{2,1,0:T(1,128)} %bitcast.21), calls=%async_computation.1 | async-start | bytes 4456448 | tf_op jit(solution)/shard_map/all_to_all | solution.py:613
  35.8 0.0 copy-done.2
  35.9 0.0 copy-done.3
  35.9 0.0 copy-start
  35.9 3.9 %levels.1 = (bf16[16,64,192]{2,1,0:T(8,128)(2,1)S(1)}, f32[16,64,64]{2,1,0:T(8,128)S(1)}, f32[8,64,64]{2,1,0:T(8,128)S(1)}, f32[4,64,128]{2,1,0:T(8,128)S(1)}) custom-call(f32[1024,128]{1,0:T(8,128)S(1)} %get-tuple-element.17.work, f32[512,128]{1,0:T(8,128)S(1)} %bitcast.41, f32[256,128]{1,0:T(8,128)S(1)} %bitcast.42), custom_call_target="tpu_custom_call" | custom-call | flops 5000000000 | bytes 2000000 | tf_op jit(solution)/shard_map/levels/pallas_call | solution.py:335
  39.8 0.0 copy-start.1
  39.8 0.0 copy-start.4
  39.8 1.6 %collective-permute-start = (f32[4,64,128]{2,1,0:T(8,128)S(1)}, f32[4,64,128]{2,1,0:T(8,128)S(1)}, u32[]{:S(2)}, u32[]{:S(2)}) collective-permute-start(f32[4,64,128]{2,1,0:T(8,128)S(1)} %get-tuple-element.21.own_ref), channel_id=1, source_target_pairs={{0,32},{32,0},{64,96},{96,64},{1,33},{33,1},{65,97},{97,65},{2,34}... | collective-permute-start | bytes 393224 | tf_op jit(solution)/shard_map/ppermute | solution.py:618
  41.5 0.0 copy-done
  41.5 2.9 %ortho.1 = f32[16,64,1024]{2,1,0:T(8,128)} custom-call(f32[1024,128]{1,0:T(8,128)S(1)} %get-tuple-element.17.work, f32[16,64,1024]{2,1,0:T(8,128)S(1)} %copy-done), custom_call_target="tpu_custom_call" | custom-call | flops 5000000000 | bytes 8000000 | tf_op jit(solution)/shard_map/ortho/pallas_call | solution.py:431
  44.4 0.0 copy-done.1
  44.4 3.4 %lefts.1 = (bf16[16,128,128]{2,1,0:T(8,128)(2,1)S(1)}, bf16[48,128,128]{2,1,0:T(8,128)(2,1)S(1)}) custom-call(s32[1,128]{1,0:T(1,128)S(1)} %bitcast.44, bf16[16,64,192]{2,1,0:T(8,128)(2,1)S(1)} %get-tuple-element.24.triple_ref, f32[4096,128]{1,0:T(8,128)S(1)} %bitcast.40), custom_call_target="tpu_custom_call" | custom-call | flops 5000000000 | bytes 6000000 | tf_op jit(solution)/shard_map/lefts/pallas_call | solution.py:474
  47.8 4.6 %level_one.1 = (f32[512,128]{1,0:T(8,128)}, f32[8,64,64]{2,1,0:T(8,128)S(1)}) custom-call(f32[8,64,64]{2,1,0:T(8,128)S(1)} %get-tuple-element.18.one_ref, f32[16,64,64]{2,1,0:T(8,128)S(1)} %get-tuple-element.19.lifted_ref, f32[256,128]{1,0:T(8,128)S(1)} %bitcast.43), custom_call_target="tpu_custom_call" | custom-call | flops 3000000000 | bytes 2000000 | tf_op jit(solution)/shard_map/level_one/pallas_call | solution.py:373
  52.5 11.1 %collective-permute-done.other_ref = f32[4,64,128]{2,1,0:T(8,128)S(1)} collective-permute-done((f32[4,64,128]{2,1,0:T(8,128)S(1)}, f32[4,64,128]{2,1,0:T(8,128)S(1)}, u32[]{:S(2)}, u32[]{:S(2)}) %collective-permute-start) | collective-permute-done | bytes 131104 | tf_op jit(solution)/shard_map/ppermute | solution.py:618
  63.6 4.2 %level_two.1 = f32[256,128]{1,0:T(8,128)} custom-call(f32[4,64,128]{2,1,0:T(8,128)S(1)} %get-tuple-element.21.own_ref, f32[4,64,128]{2,1,0:T(8,128)S(1)} %collective-permute-done.other_ref, f32[8,64,64]{2,1,0:T(8,128)S(1)} %get-tuple-element.22.raised_ref), custom_call_target="tpu_custom_call" | custom-call | flops 1000000000 | bytes 1000000 | tf_op jit(solution)/shard_map/level_two/pallas_call | solution.py:407
  67.8 0.0 all-to-all-done.1
  67.8 7.0 %finish.1 = f32[4096,128]{1,0:T(8,128)} custom-call(s32[1,128]{1,0:T(1,128)S(1)} %bitcast.46, s32[1,128]{1,0:T(1,128)S(1)} %copy-done.6, bf16[16,128,128]{2,1,0:T(8,128)(2,1)S(1)} %get-tuple-element.25.first_ref, bf16[48,128,128]{2,1,0:T(8,128)(2,1)S(1)} %get-tuple-element.26.later_hbm, f32[4352,128]{1,0:T(8,128)} %bitcast.22.pack_ref), custom_call_target="tpu_custom_call" | custom-call | flops 5000000000 | bytes 8000000 | tf_op jit(solution)/shard_map/finish/pallas_call | solution.py:577
  (5 shorter events, 0.0 us)
Async XLA Ops:
  2.2 21.2 %all-to-all-start = ((s32[128,1,128]{2,1,0:T(1,128)}), s32[128,1,128]{2,1,0:T(1,128)S(1)}, u32[]{:S(2)}, u32[]{:S(2)}) async-start(s32[128,1,128]{2,1,0:T(1,128)} %bitcast.47), calls=%async_computation | async-start | bytes 131072 | tf_op jit(solution)/shard_map/all_to_all | solution.py:610
  25.7 10.2 %copy-start.2 = (f32[16,4096]{1,0:T(8,128)S(1)}, f32[16,4096]{1,0:T(8,128)}, u32[]{:S(2)}) copy-start(f32[16,4096]{1,0:T(8,128)} %param.8) | copy-start | bytes 786436
  25.7 10.2 %copy-start.3 = (f32[8,4096]{1,0:T(8,128)S(1)}, f32[8,4096]{1,0:T(8,128)}, u32[]{:S(2)}) copy-start(f32[8,4096]{1,0:T(8,128)} %param.9) | copy-start | bytes 393220
  25.7 42.2 %all-to-all-start.1 = ((f32[128,1,4352]{2,1,0:T(1,128)}), f32[128,1,4352]{2,1,0:T(1,128)}, u32[]{:S(2)}, u32[]{:S(2)}) async-start(f32[128,1,4352]{2,1,0:T(1,128)} %bitcast.21), calls=%async_computation.1 | async-start | bytes 4456448 | tf_op jit(solution)/shard_map/all_to_all | solution.py:613
  35.9 5.6 %copy-start = (f32[16,64,1024]{2,1,0:T(8,128)S(1)}, f32[16,64,1024]{2,1,0:T(8,128)}, u32[]{:S(2)}) copy-start(f32[16,64,1024]{2,1,0:T(8,128)} %basis_ref.1) | copy-start | bytes 12582916
  39.8 4.6 %copy-start.1 = (f32[128,4096]{1,0:T(8,128)S(1)}, f32[128,4096]{1,0:T(8,128)}, u32[]{:S(2)}) copy-start(f32[128,4096]{1,0:T(8,128)} %param.10) | copy-start | bytes 6291460
  39.8 4.5 %copy-start.4 = (s32[128]{0:T(128)S(1)}, s32[128]{0:T(128)}, u32[]{:S(2)}) copy-start(s32[128]{0:T(128)} %param.11) | copy-start | bytes 1540
  39.8 23.7 %collective-permute-start = (f32[4,64,128]{2,1,0:T(8,128)S(1)}, f32[4,64,128]{2,1,0:T(8,128)S(1)}, u32[]{:S(2)}, u32[]{:S(2)}) collective-permute-start(f32[4,64,128]{2,1,0:T(8,128)S(1)} %get-tuple-element.21.own_ref), channel_id=1, source_target_pairs={{0,32},{32,0},{64,96},{96,64},{1,33},{33,1},{65,97},{97,65},{2,34}... | collective-permute-start | bytes 393224 | tf_op jit(solution)/shard_map/ppermute | solution.py:618
  52.5 15.4 %copy-start.5 = (s32[128,1]{0,1:T(1,128)S(1)}, s32[128,1]{0,1:T(1,128)}, u32[]{:S(2)}) copy-start(s32[128,1]{0,1:T(1,128)} %param.12) | copy-start | bytes 1540
  52.5 15.4 %copy-start.6 = (s32[1,128]{1,0:T(1,128)S(1)}, s32[1,128]{1,0:T(1,128)}, u32[]{:S(2)}) copy-start(s32[1,128]{1,0:T(1,128)} %get-tuple-element.23.place_ref) | copy-start | bytes 1540
